TPU v7x, 32 devices: a whole 2x2x4 slice. The times are simulated.
32 devices in a mesh: groups: 2 (over y), dp: 4 (over z), mp: 4 (over x, core).
Axes of the slice: x: 2, y: 2, z: 4, core: 2. Of those that a mesh axis runs over, the one named last changes fastest.
Arguments:
- tokens: bfloat16 [16384, 2048], P(('groups', 'dp'), 'mp'), parts along dimension 0, may hold values from -6 to 6
- x_weight: bfloat16 [2048, 2048], P(None, 'mp'), may hold values from -0.125 to 0.125
- z_weight: bfloat16 [2048, 2048], P(None, 'mp'), may hold values from -0.125 to 0.125
- bc_weight: bfloat16 [2048, 512], P(None, 'mp'), may hold values from -0.125 to 0.125
- dt_weight: bfloat16 [2048, 32], P(None, 'mp'), may hold values from -0.125 to 0.125
- dt_bias: float32 [32], P('mp'), may hold values from -3 to 1
- decay_rate: float32 [32], P('mp'), may hold values from 0.003 to 0.03
- norm_gain: float32 [2048], P('mp'), may hold values from 0.1 to 1.9
- out_weight: bfloat16 [2048, 2048], P('mp'), may hold values from -0.125 to 0.125
- store_states: bfloat16 [128, 131072], P(('groups', 'dp'), 'mp'), parts along dimension 0, may hold values from -6 to 6
- home_rows: int32 [128], P('groups'), parts along dimension 0, may hold values from 0 to 63, as said below
- event_counts: int32 [128], P(('groups', 'dp')), parts along dimension 0, may hold values from 1 to 128, as said below
Outputs:
- out_tokens: bfloat16 [16384, 2048], P(('groups', 'dp', 'mp')), parts along dimension 0
- new_store: bfloat16 [128, 131072], P(('groups', 'dp'), 'mp'), parts along dimension 0
There are 2 independent parts, one for each index of `groups`. A program takes and returns all parts, laid end to end along the dimension named above; an argument that names none is the same for every part. Nothing has to cross between parts.
Inputs may be any that keep to these rules, and one draw needn't show every extreme that they name: A permutation: session r's state is row home_rows[r] of the store. The 16 sessions of one aligned block keep at most 4 states in one aligned block of 16 store rows, and every block of sessions reaches 4 in some block of rows. `event_counts`: event slots at or after a session's count are padding.
All inputs are finite; a program needn't handle non-finite values.
Results may differ from a plain program's by a relative error of at most 0.02.
Values may be sent and summed in bfloat16 or wider, within the bound.
A program may use at most 128 MiB of HBM per device.

v0:
```python
import jax
import jax.numpy as jnp
from jax import lax
from jax.sharding import PartitionSpec as P


def pack_rows(values, wanted, slot_count):
    slots = jnp.arange(slot_count, dtype=jnp.int32)
    chosen = wanted[None, :] == slots[:, None]
    filled = jnp.any(chosen, axis=1)
    places = jnp.arange(wanted.shape[0], dtype=jnp.int32)
    source = jnp.sum(chosen.astype(jnp.int32) * places[None, :], axis=1)
    picked = jnp.take(values, source, axis=0)
    return jnp.where(filled[:, None], picked, jnp.zeros((), values.dtype))


def rank_within(keys, order):
    earlier = (keys[None, :] == keys[:, None]) & (order[None, :] < order[:, None])
    return jnp.sum(earlier.astype(jnp.int32), axis=1)


def body(
    tokens,
    x_weight,
    z_weight,
    bc_weight,
    dt_weight,
    dt_bias,
    decay_rate,
    norm_gain,
    out_weight,
    store_states,
    home_rows,
    event_counts,
):
    shard_count = lax.axis_size("dp")
    store_index = lax.axis_index("dp")
    sessions_here = store_states.shape[0]
    state_width = store_states.shape[1]
    capacity = max(2, (sessions_here + shard_count - 1) // shard_count)
    slot_count = shard_count * capacity
    local_heads = dt_bias.shape[0]
    head_size = x_weight.shape[1] // local_heads
    state_size = bc_weight.shape[1] // 2
    total_rows = tokens.shape[0]
    event_slots = total_rows // sessions_here
    positions = jnp.arange(sessions_here, dtype=jnp.int32)
    store_rows = store_index * sessions_here + positions
    everyone = jnp.arange(home_rows.shape[0], dtype=jnp.int32)
    owner = jnp.sum(
        (home_rows[None, :] == store_rows[:, None]).astype(jnp.int32) * everyone[None, :], axis=1
    )
    server = owner // sessions_here
    row_slot = server * capacity + rank_within(server, positions)
    outbound = pack_rows(store_states, row_slot, slot_count).reshape(
        shard_count, capacity, state_width
    )
    inbound = lax.all_to_all(outbound, "dp", split_axis=0, concat_axis=0, tiled=True).reshape(
        slot_count, state_width
    )
    wanted = lax.dynamic_slice_in_dim(home_rows, store_index * sessions_here, sessions_here)
    home_shard = wanted // sessions_here
    session_slot = home_shard * capacity + rank_within(home_shard, wanted % sessions_here)
    weights = (x_weight, z_weight, bc_weight, dt_weight)
    shard_cols = lax.all_gather(tokens, "mp", axis=1, tiled=True)
    x_sum, z_sum, bc_sum, dt_sum = tuple(
        (jnp.dot(shard_cols, weight, preferred_element_type=jnp.float32) for weight in weights)
    )
    initial_state = jnp.take(inbound, session_slot, axis=0).reshape(
        sessions_here, local_heads, head_size, state_size
    )
    inputs = x_sum.astype(jnp.bfloat16).reshape(sessions_here, event_slots, local_heads, head_size)
    gate_values = z_sum.astype(jnp.bfloat16)
    bc_values = bc_sum.astype(jnp.bfloat16).reshape(sessions_here, event_slots, 2 * state_size)
    b_matrix = bc_values[:, :, :state_size]
    c_matrix = bc_values[:, :, state_size:]
    valid_mask = (jnp.arange(event_slots, dtype=jnp.int32)[None, :] < event_counts[:, None]).astype(
        jnp.float32
    )
    step_sizes = (
        jax.nn.softplus(
            dt_sum.reshape(sessions_here, event_slots, local_heads) + dt_bias[None, None, :]
        )
        * valid_mask[:, :, None]
    )
    decay_sum = jnp.cumsum(step_sizes * decay_rate[None, None, :], axis=1)
    lagged = jnp.transpose(decay_sum, (0, 2, 1))
    causal_mask = jnp.arange(event_slots)[:, None] >= jnp.arange(event_slots)[None, :]
    decay_gaps = jnp.where(causal_mask, lagged[:, :, :, None] - lagged[:, :, None, :], 0.0)
    kernel = jnp.einsum("stn,sun->stu", c_matrix, b_matrix, preferred_element_type=jnp.float32)
    step_rows = jnp.transpose(step_sizes, (0, 2, 1))
    mixing = (
        jnp.where(causal_mask, jnp.exp(-decay_gaps), 0.0)
        * step_rows[:, :, None, :]
        * kernel[:, None, :, :]
    ).astype(jnp.bfloat16)
    diagonal_part = jnp.einsum(
        "shtu,suhp->sthp", mixing, inputs, preferred_element_type=jnp.float32
    )
    carried = (
        jnp.einsum("stn,shpn->sthp", c_matrix, initial_state, preferred_element_type=jnp.float32)
        * jnp.exp(-decay_sum)[:, :, :, None]
    )
    outputs = diagonal_part + carried
    final_decay = decay_sum[:, -1:, :]
    weighted = (
        b_matrix[:, :, None, :] * (jnp.exp(-(final_decay - decay_sum)) * step_sizes)[:, :, :, None]
    ).astype(jnp.bfloat16)
    new_state = (
        jnp.exp(-final_decay[:, 0, :])[:, :, None, None] * initial_state
        + jnp.einsum("suhp,suhn->shpn", inputs, weighted, preferred_element_type=jnp.float32)
    ).astype(jnp.bfloat16)
    flat_outputs = outputs.reshape(total_rows, local_heads * head_size)
    gated_values = flat_outputs * jax.nn.silu(gate_values.astype(jnp.float32))
    inverse_rms = lax.rsqrt(jnp.mean(gated_values * gated_values, axis=1, keepdims=True) + 1e-05)
    normed = (
        gated_values * inverse_rms * norm_gain[None, :] * valid_mask.reshape(total_rows, 1)
    ).astype(jnp.bfloat16)
    out_sum = lax.psum_scatter(
        jnp.dot(normed, out_weight, preferred_element_type=jnp.float32).astype(jnp.bfloat16),
        "mp",
        scatter_dimension=0,
        tiled=True,
    )
    outgoing = pack_rows(
        new_state.reshape(sessions_here, state_width), session_slot, slot_count
    ).reshape(shard_count, capacity, state_width)
    returned = lax.all_to_all(outgoing, "dp", split_axis=0, concat_axis=0, tiled=True).reshape(
        slot_count, state_width
    )
    new_store = jnp.take(returned, row_slot, axis=0)
    return (out_sum, new_store)


def solution(mesh):
    return jax.shard_map(
        body,
        mesh=mesh,
        in_specs=(
            P(("groups", "dp"), "mp"),
            P(None, "mp"),
            P(None, "mp"),
            P(None, "mp"),
            P(None, "mp"),
            P("mp"),
            P("mp"),
            P("mp"),
            P("mp", None),
            P(("groups", "dp"), "mp"),
            P("groups"),
            P(("groups", "dp")),
        ),
        out_specs=(P(("groups", "dp", "mp"), None), P(("groups", "dp"), "mp")),
        check_vma=False,
    )
```

profile of v0, /device:TPU:0, one launch (start us, length us, event | category | flops | bytes accessed | tf_op | source)
XLA Modules:
  0.0 219.1 jit_solution(15264939764608752194)
XLA Ops:
  10.2 2.2 %gather_fusion = bf16[16,32768]{1,0:T(8,128)(2,1)} fusion(bf16[16,32768]{1,0:T(8,128)(2,1)S(1)} %copy-done.1, s32[1024]{0:T(1024)S(1)} %pad_clamp_fusion.3), kind=kCustom, calls=%fused_computation.clone | custom fusion | bytes 2097216 | tf_op jit(solution)/shard_map/jit(_take)/gather | solution.py:13
  12.5 1.4 select_select_fusion.1
  15.1 6.3 %all-to-all-start = ((bf16[4,4,32768]{2,1,0:T(4,128)(2,1)}), bf16[4,4,32768]{2,1,0:T(4,128)(2,1)}, u32[]{:S(2)}, u32[]{:S(2)}) async-start(bf16[4,4,32768]{2,1,0:T(4,128)(2,1)} %reshape.181), calls=%async_computation | async-start | bytes 2097152 | tf_op jit(solution)/shard_map/all_to_all | solution.py:58
  24.9 22.3 %all-to-all-done = bf16[4,4,32768]{2,1,0:T(4,128)(2,1)} async-done(((bf16[4,4,32768]{2,1,0:T(4,128)(2,1)}), bf16[4,4,32768]{2,1,0:T(4,128)(2,1)}, u32[]{:S(2)}, u32[]{:S(2)}) %all-to-all-start) | async-done | bytes 1048608 | tf_op jit(solution)/shard_map/all_to_all | solution.py:58
  47.2 1.4 reshape.182
  48.6 2.2 %gather_fusion.1 = bf16[16,32768]{1,0:T(8,128)(2,1)} fusion(bf16[16,32768]{1,0:T(8,128)(2,1)S(1)} %reshape.182, s32[1024]{0:T(1024)S(1)} %pad_clamp_fusion.2), kind=kCustom, calls=%fused_computation.1.clone | custom fusion | bytes 2097216 | tf_op jit(solution)/shard_map/jit(_take)/gather | solution.py:69
  50.8 1.4 broadcast_select_fusion.1
  52.2 3.3 %reshape.183 = bf16[16,8,64,64]{3,2,1,0:T(8,128)(2,1)} reshape(bf16[16,32768]{1,0:T(8,128)(2,1)S(1)} %broadcast_select_fusion.1) | data formatting | bytes 2097152 | tf_op jit(solution)/shard_map/reshape | solution.py:69
  55.5 15.1 %all-gather.2.cloned.1.call-done = bf16[2048,2048]{1,0:T(8,128)(2,1)} async-done(((bf16[2048,512]{1,0:T(8,128)(2,1)}), bf16[2048,2048]{1,0:T(8,128)(2,1)}) %all-gather.2.cloned.1.call-update) | async-done | bytes 8388624 | tf_op jit(solution)/shard_map/all_gather | solution.py:65
  70.6 5.7 %broadcast_multiply_fusion = (f32[16,128,8]{1,2,0:T(8,128)S(1)}, f32[16,128,8]{1,2,0:T(8,128)S(1)}) fusion(f32[8]{0:T(128)S(1)} %copy-done.10, f32[16,128]{1,0:T(8,128)S(1)} %get-tuple-element.12, f32[8]{0:T(128)S(1)} %copy-done.11, bf16[2048,2048]{1,0:T(8,128)(2,1)} %all-gather.2.cloned.1.call-done, bf16[2048,8]{0,1:T(8,128)(2,1)S(1)} %copy-done.7), kind=kOutput, calls=%fused_computation.47 | convolution fusion | flops 67256320 | bytes 8560704 | tf_op jit(solution)/shard_map/dot_general | solution.py:67
  76.3 1.4 copy.60
  77.7 1.4 fusion.31
  80.5 5.8 %convolution_convert_fusion.3 = bf16[2048,128]{1,0:T(8,128)(2,1)S(1)} fusion(bf16[2048,2048]{1,0:T(8,128)(2,1)} %all-gather.2.cloned.1.call-done, bf16[2048,128]{1,0:T(8,128)(2,1)} %param.17), kind=kOutput, calls=%fused_computation.26 | convolution fusion | flops 1074003968 | bytes 9437184 | tf_op jit(solution)/shard_map/dot_general | solution.py:67
  87.1 1.5 fusion.18
  91.2 1.6 copy.66
  92.8 9.8 %convolution_convert_fusion.2 = bf16[2048,512]{1,0:T(8,128)(2,1)} fusion(bf16[2048,2048]{1,0:T(8,128)(2,1)} %all-gather.2.cloned.1.call-done, bf16[2048,512]{1,0:T(8,128)(2,1)} %param.15), kind=kOutput, calls=%fused_computation.25 | convolution fusion | flops 4296015872 | bytes 12582912 | tf_op jit(solution)/shard_map/dot_general | solution.py:67
  102.6 6.2 %reshape.234 = bf16[16,128,8,64]{3,2,1,0:T(8,128)(2,1)} reshape(bf16[2048,512]{1,0:T(8,128)(2,1)} %convolution_convert_fusion.2) | data formatting | bytes 4194304 | tf_op jit(solution)/shard_map/reshape | solution.py:72
  108.8 5.2 %copy.65 = bf16[16,128,8,64]{1,3,2,0:T(8,128)(2,1)} copy(bf16[16,128,8,64]{3,2,1,0:T(8,128)(2,1)} %reshape.234) | data formatting | bytes 4194304 | tf_op jit(solution)/shard_map/reshape | solution.py:72
  114.0 6.8 %fusion = f32[16,8,64,128]{3,2,1,0:T(8,128)S(1)} fusion(bf16[16,128,8,64]{1,3,2,0:T(8,128)(2,1)} %copy.65, f32[16,128,128]{2,1,0:T(8,128)S(1)} %copy-done.5, f32[16,8,128]{2,1,0:T(8,128)S(1)} %bitcast.52, f32[16,8,128]{2,1,0:T(8,128)S(1)} %copy.61, pred[128,128]{1,0:T(8,128)(4,1)S(1)} %copy-done.8), kind=kOutput, calls=%fused_computation.8 | convolution fusion | flops 283115520 | bytes 7487488 | tf_op jit(solution)/shard_map/shtu,suhp->sthp/dot_general | solution.py:97
  121.7 2.4 %copy.67 = f32[16,128,8,64]{1,0,3,2:T(8,128)S(1)} copy(f32[16,128,8,64]{1,3,2,0:T(8,128)S(1)} %bitcast_add_fusion) | data formatting | bytes 8388608 | tf_op jit(solution)/shard_map/add | solution.py:104
  124.1 9.1 %multiply_reduce_fusion = (f32[2048]{0:T(1024)S(1)}, f32[2048,512]{0,1:T(8,128)S(1)}) fusion(bf16[2048,2048]{1,0:T(8,128)(2,1)} %all-gather.2.cloned.1.call-done, bf16[2048,512]{1,0:T(8,128)(2,1)S(1)} %copy-done.19, f32[64,8,16,128]{3,2,1,0:T(8,128)S(1)} %bitcast.51), kind=kOutput, calls=%fused_computation.17 | convolution fusion | flops 4304402432 | bytes 18882560 | tf_op jit(solution)/shard_map/dot_general | solution.py:67
  133.3 7.1 %convolution_convert_fusion = bf16[2048,2048]{1,0:T(8,128)(2,1)} fusion(bf16[512,2048]{1,0:T(8,128)(2,1)S(1)} %copy-done, f32[2048,512]{0,1:T(8,128)S(1)} %get-tuple-element.16, f32[2048]{0:T(1024)S(1)} %copy-done.9, f32[512]{0:T(512)S(1)} %copy-done.20, f32[2048]{0:T(1024)S(1)} %add_rsqrt_fusion), kind=kOutput, calls=%fused_computation.5 | convolution fusion | flops 4303355904 | bytes 14698496 | tf_op jit(solution)/shard_map/dot_general | solution.py:120
  141.4 4.8 %add_convert_fusion = bf16[16,8,64,64]{3,2,1,0:T(8,128)(2,1)} fusion(bf16[16,8,64,64]{3,2,1,0:T(8,128)(2,1)} %reshape.183, bf16[16,128,8,64]{1,3,2,0:T(8,128)(2,1)} %copy.65, f32[16,128,8]{1,2,0:T(8,128)S(1)} %exponential_multiply_fusion, f32[16,128,64]{1,2,0:T(8,128)S(1)} %copy-done.6, f32[16,8]{1,0:T(8,128)S(1)} %copy.69), kind=kOutput, calls=%fused_computation.14 | convolution fusion | flops 138412032 | bytes 4784640 | tf_op jit(solution)/shard_map/suhp,suhn->shpn/dot_general | solution.py:111
  146.2 2.9 %reshape.185 = bf16[16,32768]{1,0:T(8,128)(2,1)S(1)} reshape(bf16[16,8,64,64]{3,2,1,0:T(8,128)(2,1)} %add_convert_fusion) | data formatting | bytes 2097152 | tf_op jit(solution)/shard_map/reshape | solution.py:126
  149.1 2.3 %gather_fusion.2 = bf16[16,32768]{1,0:T(8,128)(2,1)} fusion(bf16[16,32768]{1,0:T(8,128)(2,1)S(1)} %reshape.185, s32[1024]{0:T(1024)} %pad_clamp_fusion.1), kind=kCustom, calls=%fused_computation.2.clone | custom fusion | bytes 2097216 | tf_op jit(solution)/shard_map/jit(_take)/gather | solution.py:13
  151.5 1.6 select_select_fusion
  154.3 4.6 %all-to-all-start.1 = ((bf16[4,4,32768]{2,1,0:T(4,128)(2,1)}), bf16[4,4,32768]{2,1,0:T(4,128)(2,1)}, u32[]{:S(2)}, u32[]{:S(2)}) async-start(bf16[4,4,32768]{2,1,0:T(4,128)(2,1)} %reshape.186), calls=%async_computation.2 | async-start | bytes 2097152 | tf_op jit(solution)/shard_map/all_to_all | solution.py:128
  158.9 26.2 %all-to-all-done.1 = bf16[4,4,32768]{2,1,0:T(4,128)(2,1)} async-done(((bf16[4,4,32768]{2,1,0:T(4,128)(2,1)}), bf16[4,4,32768]{2,1,0:T(4,128)(2,1)}, u32[]{:S(2)}, u32[]{:S(2)}) %all-to-all-start.1) | async-done | bytes 1048608 | tf_op jit(solution)/shard_map/all_to_all | solution.py:128
  185.1 1.4 reshape.187
  186.5 2.2 %gather_fusion.3 = bf16[16,32768]{1,0:T(8,128)(2,1)} fusion(bf16[16,32768]{1,0:T(8,128)(2,1)S(1)} %reshape.187, s32[1024]{0:T(1024)S(1)} %pad_clamp_fusion), kind=kCustom, calls=%fused_computation.3.clone | custom fusion | bytes 2097216 | tf_op jit(solution)/shard_map/jit(_take)/gather | solution.py:131
  188.7 2.4 %broadcast_select_fusion = bf16[16,32768]{1,0:T(8,128)(2,1)} fusion(bf16[16,32768]{1,0:T(8,128)(2,1)} %gather_fusion.3, pred[16]{0:T(512)(128)(4,1)S(1)} %copy-done.12), kind=kLoop, calls=%fused_computation.37 | loop fusion | flops 524288 | bytes 2097168 | tf_op jit(solution)/shard_map/jit(_take)/select_n | solution.py:131
  191.1 21.2 %reduce-scatter.2.cloned.1.call-done = bf16[512,2048]{1,0:T(8,128)(2,1)} async-done(((bf16[2048,2048]{1,0:T(8,128)(2,1)}), bf16[512,2048]{1,0:T(8,128)(2,1)}) %reduce-scatter.2.cloned.1.call-update) | async-done | bytes 2097168 | tf_op jit(solution)/shard_map/reduce_scatter | solution.py:119
  (85 shorter events, 15.8 us)
Async XLA Ops:
  7.2 126.1 %copy-start = (bf16[512,2048]{1,0:T(8,128)(2,1)S(1)}, bf16[512,2048]{1,0:T(8,128)(2,1)}, u32[]{:S(2)}) copy-start(bf16[512,2048]{1,0:T(8,128)(2,1)} %param.22) | copy-start | bytes 6291460
  7.2 3.1 %copy-start.1 = (bf16[16,32768]{1,0:T(8,128)(2,1)S(1)}, bf16[16,32768]{1,0:T(8,128)(2,1)}, u32[]{:S(2)}) copy-start(bf16[16,32768]{1,0:T(8,128)(2,1)} %param.23) | copy-start | bytes 3145732
  7.2 63.4 %all-gather.2.cloned.1.call-start = ((), (), s32[]{:S(2)}) async-start(), calls=%async_computation.3 | async-start | bytes 10485760 | tf_op jit(solution)/shard_map/all_gather | solution.py:65
  9.6 0.5 copy-start.15
  12.5 9.0 %copy-start.14 = (s32[64]{0:T(128)S(1)}, s32[64]{0:T(128)}, u32[]{:S(2)}) copy-start(s32[64]{0:T(128)} %param.24) | copy-start | bytes 772
  12.5 11.8 %copy-start.13 = (s32[16]{0:T(128)S(1)}, s32[16]{0:T(128)}, u32[]{:S(2)}) copy-start(s32[16]{0:T(128)} %param.25) | copy-start | bytes 196
  15.1 32.1 %all-to-all-start = ((bf16[4,4,32768]{2,1,0:T(4,128)(2,1)}), bf16[4,4,32768]{2,1,0:T(4,128)(2,1)}, u32[]{:S(2)}, u32[]{:S(2)}) async-start(bf16[4,4,32768]{2,1,0:T(4,128)(2,1)} %reshape.181), calls=%async_computation | async-start | bytes 2097152 | tf_op jit(solution)/shard_map/all_to_all | solution.py:58
  21.4 190.9 %reduce-scatter.2.cloned.1.call-start = ((), (), s32[]{:S(2)}) async-start(), calls=%async_computation.4 | async-start | bytes 10485760 | tf_op jit(solution)/shard_map/reduce_scatter | solution.py:119
  50.8 19.8 %copy-start.7 = (bf16[2048,8]{0,1:T(8,128)(2,1)S(1)}, bf16[2048,8]{0,1:T(8,128)(2,1)}, u32[]{:S(2)}) copy-start(bf16[2048,8]{0,1:T(8,128)(2,1)} %param.18) | copy-start | bytes 98308
  50.8 19.8 %copy-start.10 = (f32[8]{0:T(128)S(1)}, f32[8]{0:T(128)}, u32[]{:S(2)}) copy-start(f32[8]{0:T(128)} %param.20) | copy-start | bytes 100
  50.8 19.8 %copy-start.11 = (f32[8]{0:T(128)S(1)}, f32[8]{0:T(128)}, u32[]{:S(2)}) copy-start(f32[8]{0:T(128)} %param.19) | copy-start | bytes 100
  86.3 0.8 copy-start.3
  108.8 5.2 %copy-start.5 = (f32[16,128,128]{2,1,0:T(8,128)S(1)}, f32[16,128,128]{2,1,0:T(8,128)}, u32[]{:S(2)}) copy-start(f32[16,128,128]{2,1,0:T(8,128)} %fusion.18) | copy-start | bytes 3145732
  108.8 5.2 %copy-start.8 = (pred[128,128]{1,0:T(8,128)(4,1)S(1)}, pred[128,128]{1,0:T(8,128)(4,1)}, u32[]{:S(2)}) copy-start(pred[128,128]{1,0:T(8,128)(4,1)} %iota_compare_fusion) | copy-start | bytes 49156
  114.0 6.8 %copy-start.2 = (bf16[16,8,64,64]{3,2,1,0:T(8,128)(2,1)S(1)}, bf16[16,8,64,64]{3,2,1,0:T(8,128)(2,1)}, u32[]{:S(2)}) copy-start(bf16[16,8,64,64]{3,2,1,0:T(8,128)(2,1)} %reshape.183) | copy-start | bytes 3145732
  114.0 6.8 %copy-start.4 = (bf16[2048,128]{1,0:T(8,128)(2,1)S(1)}, bf16[2048,128]{1,0:T(8,128)(2,1)}, u32[]{:S(2)}) copy-start(bf16[2048,128]{1,0:T(8,128)(2,1)} %copy-done.3) | copy-start | bytes 1572868
  121.7 2.4 %copy-start.19 = (bf16[2048,512]{1,0:T(8,128)(2,1)S(1)}, bf16[2048,512]{1,0:T(8,128)(2,1)}, u32[]{:S(2)}) copy-start(bf16[2048,512]{1,0:T(8,128)(2,1)} %param.16) | copy-start | bytes 6291460
  124.1 9.2 %copy-start.9 = (f32[2048]{0:T(1024)S(1)}, f32[2048]{0:T(1024)}, u32[]{:S(2)}) copy-start(f32[2048]{0:T(1024)} %get-tuple-element.11) | copy-start | bytes 24580
  124.1 9.2 %copy-start.20 = (f32[512]{0:T(512)S(1)}, f32[512]{0:T(512)}, u32[]{:S(2)}) copy-start(f32[512]{0:T(512)} %param.21) | copy-start | bytes 6148
  140.4 1.0 copy-start.6
  149.1 2.4 %copy-start.17 = (pred[16]{0:T(512)(128)(4,1)S(1)}, pred[16]{0:T(512)(128)(4,1)}, u32[]{:S(2)}) copy-start(pred[16]{0:T(512)(128)(4,1)} %fusion.22) | copy-start | bytes 52
  149.1 2.3 %copy-start.18 = (pred[16]{0:T(512)(128)(4,1)S(1)}, pred[16]{0:T(512)(128)(4,1)}, u32[]{:S(2)}) copy-start(pred[16]{0:T(512)(128)(4,1)} %compare_and_fusion.1) | copy-start | bytes 52
  151.4 7.5 %copy-start.16 = (s32[16]{0:T(128)S(1)}, s32[16]{0:T(128)}, u32[]{:S(2)}) copy-start(s32[16]{0:T(128)} %copy-done.15) | copy-start | bytes 196
  154.3 30.8 %all-to-all-start.1 = ((bf16[4,4,32768]{2,1,0:T(4,128)(2,1)}), bf16[4,4,32768]{2,1,0:T(4,128)(2,1)}, u32[]{:S(2)}, u32[]{:S(2)}) async-start(bf16[4,4,32768]{2,1,0:T(4,128)(2,1)} %reshape.186), calls=%async_computation.2 | async-start | bytes 2097152 | tf_op jit(solution)/shard_map/all_to_all | solution.py:128
  186.5 2.2 %copy-start.12 = (pred[16]{0:T(512)(128)(4,1)S(1)}, pred[16]{0:T(512)(128)(4,1)}, u32[]{:S(2)}) copy-start(pred[16]{0:T(512)(128)(4,1)} %get-tuple-element.3) | copy-start | bytes 52
Sparse Core Ops, SparseCore 0:
  9.6 60.9 all-gather.1
  140.5 71.7 reduce-scatter.1
where the time goes:
time: 220 us; the launch traced here: 219 us
  waiting for transfers between devices  85.5 us (39%)
  matrix products  51.4 us (23%)
  local copies, waits for them, and re-layouts  41.3 us (19%)
  other arithmetic  15.7 us (7%)
  between operations  14.3 us (6%)
  starting transfers between devices  11 us (5%)
    dot_general x4, matrix products, body(): jnp.dot(shard_cols, weight, preferred_element_type=jnp.float32)  30.4 us
    all_to_all x1, waiting for transfers between devices, body(): lax.all_to_all(outgoing, 'dp', split_axis=0, concat_axis=0, tiled=True)  26.2 us
    all_to_all x1, waiting for transfers between devices, body(): lax.all_to_all(outbound, 'dp', split_axis=0, concat_axis=0, tiled=True)  22.3 us
    reduce_scatter x1, waiting for transfers between devices, body(): lax.psum_scatter(jnp.dot(normed, out_weight, preferred_element_type=jnp.f...  21.2 us
    all_gather x1, waiting for transfers between devices, body(): shard_cols = lax.all_gather(tokens, 'mp', axis=1, tiled=True)  15.1 us
    reshape x2, local copies, waits for them, and re-layouts, body(): x_sum.astype(jnp.bfloat16)  11.4 us
    dot_general x1, matrix products, body(): jnp.dot(normed, out_weight, preferred_element_type=jnp.float32)  7.08 us
    dot_general x1, matrix products, body(): jnp.einsum('shtu,suhp->sthp', mixing, inputs, preferred_element_type=jnp....  6.77 us
  transfers between devices with their start and end apart: 4, of which 4 were waited for; matrix products, arithmetic and copies ran while one was open for 17% of the time, Pallas kernels for 0%

commit v1 on v0

v1 whole, which is shorter than its diff:
```python
import functools

import jax
import jax.numpy as jnp
from jax import lax
from jax.experimental import pallas as pl
from jax.experimental.pallas import tpu as pltpu
from jax.sharding import PartitionSpec as P

F32 = jnp.float32
BF16 = jnp.bfloat16


def rank_within(keys, order):
    earlier = (keys[None, :] == keys[:, None]) & (order[None, :] < order[:, None])
    return jnp.sum(earlier.astype(jnp.int32), axis=1)


def one_hot_rows(wanted, count):
    places = jnp.arange(count, dtype=jnp.int32)
    return (wanted[:, None] == places[None, :]).astype(BF16)


def chunk_kernel(
    heads,
    head_size,
    state_size,
    scalars,
    own_ref,
    sib_ref,
    far_ref,
    diag_ref,
    weight_ref,
    bias_ref,
    rate_ref,
    gain_ref,
    start_ref,
    normed_ref,
    state_ref,
    acc_ref,
):
    parts = own_ref.shape[0]
    slots = own_ref.shape[2]
    depth = own_ref.shape[3]
    inner = heads * head_size
    me = scalars[0]
    total = None
    for step, ref in enumerate((own_ref, sib_ref, far_ref, diag_ref)):
        rows = pl.ds(pl.multiple_of(jnp.bitwise_xor(me, step) * depth, depth), depth)
        piece = jnp.dot(
            ref[...].reshape(parts * slots, depth),
            weight_ref[rows, :],
            preferred_element_type=F32,
        )
        total = piece if total is None else total + piece
    acc_ref[...] = total

    lane = lax.broadcasted_iota(jnp.int32, (slots, slots), 1)
    row = lax.broadcasted_iota(jnp.int32, (slots, slots), 0)
    causal = row >= lane
    low = lane < head_size
    lane8 = lax.broadcasted_iota(jnp.int32, (heads, slots), 1)
    pair = 2 * head_size

    for step in range(parts):
        place = jnp.bitwise_xor(me, step)
        here = pl.ds(pl.multiple_of(place * slots, slots), slots)
        count = scalars[1 + step]
        slab = acc_ref[here, 2 * inner : 2 * inner + 128]
        b_f32 = slab[:, :state_size].astype(BF16).astype(F32)
        b_bf = slab[:, :state_size].astype(BF16)
        c_bf = acc_ref[here, 2 * inner + 128 : 2 * inner + 128 + state_size].astype(BF16)
        raw = slab.T[state_size : state_size + heads, :] + bias_ref[...]
        dt_t = jnp.maximum(raw, 0.0) + jnp.log1p(jnp.exp(-jnp.abs(raw)))
        dt_t = jnp.where(lane8 < count, dt_t, 0.0)
        cum_t = dt_t * rate_ref[...]
        shift = 1
        while shift < slots:
            moved = pltpu.roll(cum_t, shift, axis=1)
            cum_t = cum_t + jnp.where(lane8 >= shift, moved, 0.0)
            shift *= 2
        last = cum_t[:, slots - 1 : slots]
        weigh_t = jnp.exp(cum_t - last) * dt_t
        fade_t = jnp.exp(-cum_t)
        stacked = jnp.concatenate(
            [cum_t, weigh_t, fade_t, jnp.zeros((slots - 3 * heads, slots), F32)], axis=0
        ).T
        scores = lax.dot_general(
            c_bf, b_bf, (((1,), (1,)), ((), ())), preferred_element_type=F32
        )
        gated_parts = []
        squares = None
        for j in range(heads // 2):
            cols = slice(j * pair, (j + 1) * pair)
            xs = acc_ref[here, cols].astype(BF16)
            zs = acc_ref[here, inner + j * pair : inner + (j + 1) * pair].astype(BF16).astype(F32)
            split = jnp.concatenate(
                [jnp.where(low, xs, jnp.zeros((), BF16)), jnp.where(low, jnp.zeros((), BF16), xs)],
                axis=0,
            )
            mixes = []
            weighed = []
            for h in (2 * j, 2 * j + 1):
                gaps = jnp.where(causal, cum_t[h : h + 1, :] - stacked[:, h : h + 1], -1e30)
                mixes.append((jnp.exp(gaps) * dt_t[h : h + 1, :] * scores).astype(BF16))
                weighed.append((b_f32 * stacked[:, heads + h : heads + h + 1]).astype(BF16))
            y = jnp.dot(jnp.concatenate(mixes, axis=1), split, preferred_element_type=F32)
            start = start_ref[step, cols, :]
            carried = lax.dot_general(
                c_bf, start, (((1,), (1,)), ((), ())), preferred_element_type=F32
            )
            fade0 = stacked[:, 2 * heads + 2 * j : 2 * heads + 2 * j + 1]
            fade1 = stacked[:, 2 * heads + 2 * j + 1 : 2 * heads + 2 * j + 2]
            y = y + carried * jnp.where(low, fade0, fade1)
            grown = lax.dot_general(
                split,
                jnp.concatenate(weighed, axis=0),
                (((0,), (0,)), ((), ())),
                preferred_element_type=F32,
            )
            keep = jnp.where(
                row[:, :state_size] < head_size,
                fade_t[2 * j : 2 * j + 1, slots - 1 : slots],
                fade_t[2 * j + 1 : 2 * j + 2, slots - 1 : slots],
            )
            state_ref[step, cols, :] = (keep * start.astype(F32) + grown).astype(BF16)
            gated = y * (zs * jax.nn.sigmoid(zs))
            part = jnp.sum(gated * gated, axis=1, keepdims=True)
            squares = part if squares is None else squares + part
            gated_parts.append(gated)
        scale = lax.rsqrt(squares * (1.0 / inner) + 1e-05)
        scale = jnp.where(row[:, :1] < count, scale, 0.0)
        for j in range(heads // 2):
            cols = slice(j * pair, (j + 1) * pair)
            normed_ref[step, :, cols] = (gated_parts[j] * scale * gain_ref[:, cols]).astype(BF16)


def run_chunk(index, scalars, tokens4, sib, far, diag, weight, bias, rate, gain, start, heads, head_size, state_size):
    parts, _, slots, depth = tokens4.shape
    inner = heads * head_size
    width = weight.shape[1]
    chunk = pl.BlockSpec((parts, 1, slots, depth), lambda i, s: (0, 0, 0, 0))
    whole = lambda shape: pl.BlockSpec(shape, lambda i, s: (0,) * len(shape))
    rows = parts * slots
    return pl.pallas_call(
        functools.partial(chunk_kernel, heads, head_size, state_size),
        out_shape=(
            jax.ShapeDtypeStruct((parts, slots, inner), BF16),
            jax.ShapeDtypeStruct((parts, inner, state_size), BF16),
        ),
        grid_spec=pltpu.PrefetchScalarGridSpec(
            num_scalar_prefetch=1,
            grid=(1,),
            in_specs=[
                pl.BlockSpec((parts, 1, slots, depth), lambda i, s: (0, index, 0, 0)),
                chunk,
                chunk,
                chunk,
                whole(weight.shape),
                whole(bias.shape),
                whole(rate.shape),
                whole(gain.shape),
                pl.BlockSpec((parts, inner, state_size), lambda i, s: (index, 0, 0)),
            ],
            out_specs=(
                whole((parts, slots, inner)),
                whole((parts, inner, state_size)),
            ),
            scratch_shapes=[pltpu.VMEM((rows, width), F32)],
        ),
        compiler_params=pltpu.CompilerParams(vmem_limit_bytes=48 * 1024 * 1024),
        cost_estimate=pl.CostEstimate(
            flops=2 * rows * 4 * depth * width * 2,
            bytes_accessed=12 * 1024 * 1024,
            transcendentals=rows * heads * slots,
        ),
        name="chunk_layer",
    )(scalars, tokens4, sib, far, diag, weight, bias, rate, gain, start)


def body(
    tokens,
    x_weight,
    z_weight,
    bc_weight,
    dt_weight,
    dt_bias,
    decay_rate,
    norm_gain,
    out_weight,
    store_states,
    home_rows,
    event_counts,
):
    shard_count = lax.axis_size("dp")
    replica_count = lax.axis_size("groups")
    parts = lax.axis_size("mp")
    me = lax.axis_index("dp")
    part = lax.axis_index("mp").astype(jnp.int32)
    sessions = store_states.shape[0]
    state_width = store_states.shape[1]
    capacity = max(2, (sessions + shard_count - 1) // shard_count)
    slot_count = shard_count * capacity
    heads = dt_bias.shape[0]
    inner = x_weight.shape[1]
    head_size = inner // heads
    state_size = bc_weight.shape[1] // 2
    model = x_weight.shape[0]
    depth = tokens.shape[1]
    slots = tokens.shape[0] // sessions
    chunks = sessions // parts

    def swap(values, mask):
        return lax.ppermute(values, "mp", [(i, i ^ mask) for i in range(parts)])

    def shift_exchange(blocks):
        arrived = [blocks[0]]
        for k in range(1, shard_count):
            perm = [(i, (i + k) % shard_count) for i in range(shard_count)]
            arrived.append(lax.ppermute(blocks[k], "dp", perm))
        return jnp.concatenate(arrived, axis=0)

    tokens4 = tokens.reshape(parts, chunks, slots, depth)
    far_pieces = [swap(tokens4[:, j : j + 1], 2) for j in range(chunks)]

    positions = jnp.arange(sessions, dtype=jnp.int32)
    store_rows = me * sessions + positions
    everyone = jnp.arange(home_rows.shape[0], dtype=jnp.int32)
    owner = jnp.sum(
        (home_rows[None, :] == store_rows[:, None]).astype(jnp.int32) * everyone[None, :], axis=1
    )
    server = owner // sessions
    to_server = (server - me + shard_count) % shard_count
    row_slot = to_server * capacity + rank_within(server, positions)
    back_slot = row_slot
    wanted = lax.dynamic_slice_in_dim(home_rows, me * sessions, sessions)
    home_shard = wanted // sessions
    from_home = (me - home_shard + shard_count) % shard_count
    session_slot = from_home * capacity + rank_within(home_shard, wanted % sessions)

    pack = one_hot_rows(row_slot, slot_count).T
    outbound = jnp.dot(pack, store_states, preferred_element_type=F32).astype(BF16)
    inbound = shift_exchange(
        [outbound[k * capacity : (k + 1) * capacity] for k in range(shard_count)]
    )
    spots = jnp.arange(sessions, dtype=jnp.int32)
    chunk_order = jnp.bitwise_xor(spots % parts, part) * chunks + spots // parts
    unpack = one_hot_rows(session_slot[chunk_order], slot_count)
    start = (
        jnp.dot(unpack, inbound, preferred_element_type=F32)
        .astype(BF16)
        .reshape(sessions, inner, state_size)
    )

    pad_b = jnp.zeros((model, 128 - state_size - heads), BF16)
    pad_c = jnp.zeros((model, 128 - state_size), BF16)
    weight = jnp.concatenate(
        [
            x_weight,
            z_weight,
            bc_weight[:, :state_size],
            dt_weight,
            pad_b,
            bc_weight[:, state_size:],
            pad_c,
        ],
        axis=1,
    )
    ordered_counts = event_counts[chunk_order]

    replicas = replica_count * shard_count
    piece_rows = out_weight.shape[0] // replicas
    replica = lax.axis_index("groups") * shard_count + me
    piece = lax.dynamic_slice_in_dim(out_weight, replica * piece_rows, piece_rows, 0)
    piece = swap(piece, 2)
    far_out = lax.all_gather(piece, ("groups", "dp"), axis=0, tiled=True)
    sib_out = swap(out_weight, 1)
    diag_out = swap(far_out, 1)

    received = [[] for _ in range(parts)]
    states = []
    for j in range(chunks):
        far = far_pieces[j]
        sib = swap(tokens4[:, j : j + 1], 1)
        diag = swap(far, 1)
        scalars = jnp.concatenate([part[None], ordered_counts[j * parts : (j + 1) * parts]])
        normed, state = run_chunk(
            j,
            scalars,
            tokens4,
            sib,
            far,
            diag,
            weight,
            dt_bias[:, None],
            decay_rate[:, None],
            norm_gain[None, :],
            start,
            heads,
            head_size,
            state_size,
        )
        states.append(state)
        received[0].append(normed[0])
        for k in range(1, parts):
            received[k].append(swap(normed[k], k))
    new_state = jnp.concatenate(states, axis=0).reshape(sessions, state_width)
    slot_of = one_hot_rows(session_slot[chunk_order], slot_count).T
    outgoing = jnp.dot(slot_of, new_state, preferred_element_type=F32).astype(BF16)
    back = [outgoing[k * capacity : (k + 1) * capacity] for k in range(shard_count)]
    arrived = [back[0]]
    for k in range(1, shard_count):
        perm = [(i, (i - k) % shard_count) for i in range(shard_count)]
        arrived.append(lax.ppermute(back[k], "dp", perm))
    returned = jnp.concatenate(arrived, axis=0)
    new_store = jnp.dot(
        one_hot_rows(back_slot, slot_count), returned, preferred_element_type=F32
    ).astype(BF16)

    mixed = jnp.concatenate([jnp.concatenate(blocks, axis=0) for blocks in received], axis=1)
    out_full = jnp.concatenate([out_weight, sib_out, far_out, diag_out], axis=0)
    out_sum = jnp.dot(mixed, out_full, preferred_element_type=F32).astype(BF16)
    return (out_sum, new_store)


def solution(mesh):
    return jax.shard_map(
        body,
        mesh=mesh,
        in_specs=(
            P(("groups", "dp"), "mp"),
            P(None, "mp"),
            P(None, "mp"),
            P(None, "mp"),
            P(None, "mp"),
            P("mp"),
            P("mp"),
            P("mp"),
            P("mp", None),
            P(("groups", "dp"), "mp"),
            P("groups"),
            P(("groups", "dp")),
        ),
        out_specs=(P(("groups", "dp", "mp"), None), P(("groups", "dp"), "mp")),
        check_vma=False,
    )
```

time: 220 us -> 177 us (0.80)
  Pallas kernels: 0 us -> 42.7 us
  waiting for transfers between devices: 85.5 us -> 46.7 us
  matrix products: 51.4 us -> 16.3 us
  other arithmetic: 15.7 us -> 2.81 us
  starting transfers between devices: 11 us -> 22.3 us
  local copies, waits for them, and re-layouts: 41.3 us -> 31 us
    all_to_all x2 -> x0, waiting for transfers between devices: 48.5 us -> none  [the longest x1 26.2 us: body(): lax.all_to_all(outgoing, 'dp', split_axis=0, concat_axis=0, tiled=True)]
    ppermute x0 -> x33, waiting for transfers between devices: none -> 46.7 us  [the longest x3 20.8 us: body(): arrived.append(lax.ppermute(back[k], 'dp', perm))]
    pallas_call x0 -> x4, Pallas kernels: none -> 42.7 us  [run_chunk(): pl.pallas_call(functools.partial(chunk_kernel, heads, head_size, state_si...]
    dot_general x9 -> x5, matrix products: 51.4 us -> 16.3 us  [the longest x1 9.58 us: body(): out_sum = jnp.dot(mixed, out_full, preferred_element_type=F32).astype(BF16)]
    ppermute x0 -> x33, starting transfers between devices: none -> 22.2 us  [the longest x27 16 us: swap(): return lax.ppermute(values, 'mp', [(i, i ^ mask) for i in range(parts)])]
    reduce_scatter x1 -> x0, waiting for transfers between devices: 21.2 us -> none  [body(): lax.psum_scatter(jnp.dot(normed, out_weight, preferred_element_type=jnp.f...]
    reshape x8 -> x2, local copies, waits for them, and re-layouts: 22.7 us -> 7.34 us  [the longest x1 4.18 us: body(): start = jnp.dot(unpack, inbound, preferred_element_type=F32).astype(BF16)...]
    all_gather x1, waiting for transfers between devices: 15.1 us -> 0.01 us  [body(): far_out = lax.all_gather(piece, ('groups', 'dp'), axis=0, tiled=True)]
  transfers between devices with their start and end apart: 4 -> 34, of which waited for: 4 -> 11; matrix products, arithmetic and copies ran while one was open for 17% -> 18% of each run, Pallas kernels for 0% -> 24%
where the time goes in v1:
time: 177 us; the launch traced here: 176 us
  waiting for transfers between devices  46.7 us (26%)
  Pallas kernels  42.7 us (24%)
  local copies, waits for them, and re-layouts  31 us (18%)
  starting transfers between devices  22.3 us (13%)
  matrix products  16.3 us (9%)
  between operations  14.4 us (8%)
  other arithmetic  2.81 us (2%)
    pallas_call x4, Pallas kernels, run_chunk(): pl.pallas_call(functools.partial(chunk_kernel, heads, head_size, state_si...  42.7 us
    ppermute x3, waiting for transfers between devices, body(): arrived.append(lax.ppermute(back[k], 'dp', perm))  20.8 us
    ppermute x27, starting transfers between devices, swap(): return lax.ppermute(values, 'mp', [(i, i ^ mask) for i in range(parts)])  16 us
    ppermute x3, waiting for transfers between devices, shift_exchange(): arrived.append(lax.ppermute(blocks[k], 'dp', perm))  13.5 us
    ppermute x27, waiting for transfers between devices, swap(): return lax.ppermute(values, 'mp', [(i, i ^ mask) for i in range(parts)])  12.4 us
    dot_general x1, matrix products, body(): out_sum = jnp.dot(mixed, out_full, preferred_element_type=F32).astype(BF16)  9.58 us
    concatenate x1, local copies, waits for them, and re-layouts, body(): jnp.concatenate([x_weight, z_weight, bc_weight[:, :state_size], dt_weight...  9.23 us
    unnamed x65, local copies, waits for them, and re-layouts  6.06 us
  transfers between devices with their start and end apart: 34, of which 11 were waited for; matrix products, arithmetic and copies ran while one was open for 18% of the time, Pallas kernels for 24%

profile of v1, /device:TPU:0, one launch (start us, length us, event | category | flops | bytes accessed | tf_op | source)
XLA Modules:
  0.0 176.2 jit_solution(15559812731258701005)
XLA Ops:
  7.2 3.0 %fusion.74 = (bf16[4,1,128,512]{3,2,1,0:T(8,128)(2,1)}, bf16[4,1,128,512]{3,2,1,0:T(8,128)(2,1)}, bf16[4,1,128,512]{3,2,1,0:T(8,128)(2,1)}, bf16[4,1,128,512]{3,2,1,0:T(8,128)(2,1)}) fusion(bf16[4,4,128,512]{3,2,1,0:T(8,128)(2,1)} %bitcast.41), kind=kLoop, calls=%fused_computation.128 | loop fusion | bytes 4194304 | tf_op jit(solution)/shard_map/slice | solution.py:284
  10.2 2.9 %collective-permute-start.1 = (bf16[4,1,128,512]{3,2,1,0:T(8,128)(2,1)}, bf16[4,1,128,512]{3,2,1,0:T(8,128)(2,1)}, u32[]{:S(2)}, u32[]{:S(2)}) collective-permute-start(bf16[4,1,128,512]{3,2,1,0:T(8,128)(2,1)} %get-tuple-element.20), channel_id=1, source_target_pairs={{0,2},{1,3},{2,0},{3,1},{4,6},{5,7},{6,4},{7,5},{8,10},{9,11},{10,... | collective-permute-start | bytes 1572872 | tf_op jit(solution)/shard_map/ppermute | solution.py:214
  14.1 1.1 fusion.76
  15.3 1.6 collective-permute-start.3
  16.8 2.6 %collective-permute-start.4 = (bf16[4,32768]{1,0:T(4,128)(2,1)S(1)}, bf16[4,32768]{1,0:T(4,128)(2,1)}, u32[]{:S(2)}, u32[]{:S(2)}) collective-permute-start(bf16[4,32768]{1,0:T(4,128)(2,1)S(1)} %get-tuple-element.30), channel_id=1, source_target_pairs={{0,8},{4,12},{8,0},{12,4},{1,9},{5,13},{9,1},{13,5},{2,10},{6,14},... | collective-permute-start | bytes 786440 | tf_op jit(solution)/shard_map/ppermute | solution.py:220
  21.9 1.2 fusion.77
  23.3 3.0 %collective-permute-done.3 = bf16[4,32768]{1,0:T(4,128)(2,1)} collective-permute-done((bf16[4,32768]{1,0:T(4,128)(2,1)S(1)}, bf16[4,32768]{1,0:T(4,128)(2,1)}, u32[]{:S(2)}, u32[]{:S(2)}) %collective-permute-start.3) | collective-permute-done | bytes 262176 | tf_op jit(solution)/shard_map/ppermute | solution.py:220
  26.8 10.4 %collective-permute-done.4 = bf16[4,32768]{1,0:T(4,128)(2,1)} collective-permute-done((bf16[4,32768]{1,0:T(4,128)(2,1)S(1)}, bf16[4,32768]{1,0:T(4,128)(2,1)}, u32[]{:S(2)}, u32[]{:S(2)}) %collective-permute-start.4) | collective-permute-done | bytes 262176 | tf_op jit(solution)/shard_map/ppermute | solution.py:220
  37.2 1.6 collective-permute-start.5
  40.7 9.2 %concatenate.43.weight_ref = bf16[2048,1280]{1,0:T(8,128)(2,1)} concatenate(bf16[2048,512]{1,0:T(8,128)(2,1)} %param.13, bf16[2048,512]{1,0:T(8,128)(2,1)} %param.14, bf16[2048,64]{1,0:T(8,128)(2,1)} %get-tuple-element.49, bf16[2048,8]{1,0:T(8,128)(2,1)S(1)} %copy.32, bf16[2048,56]{1,0:T(8,128)(2,1)S(1)} %broadcast_in_dim.13, bf16[2048,64]{1,0:T(8,128)(2,1)} %get-tuple-element.48, ...), dimensions={1} | concatenate | bytes 10485760 | tf_op jit(solution)/shard_map/concatenate | solution.py:257
  51.4 1.5 collective-permute-start.13
  52.9 2.9 %convolution_convert_fusion.2 = bf16[16,32768]{1,0:T(8,128)(2,1)} fusion(bf16[4,32768]{1,0:T(4,128)(2,1)} %collective-permute-done.5, bf16[4,32768]{1,0:T(4,128)(2,1)} %collective-permute-done.4, bf16[4,32768]{1,0:T(4,128)(2,1)} %collective-permute-done.3, bf16[4,32768]{1,0:T(4,128)(2,1)} %get-tuple-element.28, s32[16]{0:T(128)S(1)} %gather_fusion.1), kind=kOutput, calls=%fused_computation.4 | convolution fusion | flops 21496064 | bytes 2097216 | tf_op jit(solution)/shard_map/dot_general | solution.py:250
  55.9 4.2 %reshape.144.start_ref = bf16[16,512,64]{2,1,0:T(8,128)(2,1)} reshape(bf16[16,32768]{1,0:T(8,128)(2,1)} %convolution_convert_fusion.2) | data formatting | bytes 2097152 | tf_op jit(solution)/shard_map/reshape | solution.py:252
  60.6 1.0 copy-done.11
  61.7 10.6 %chunk_layer.4 = (bf16[4,128,512]{2,1,0:T(8,128)(2,1)S(1)}, bf16[4,512,64]{2,1,0:T(8,128)(2,1)S(1)}) custom-call(s32[5]{0:T(128)S(1)} %pad_add_fusion.scalars, bf16[4,4,128,512]{3,2,1,0:T(8,128)(2,1)S(1)} %bitcast.42, bf16[4,1,128,512]{3,2,1,0:T(8,128)(2,1)S(1)} %copy-done.11, bf16[4,1,128,512]{3,2,1,0:T(8,128)(2,1)} %collective-permute-done.1.far_ref, ...), custom_call_target="tpu_custom_call" | custom-call | flops 5368709120 | bytes 12582912 | tf_op jit(solution)/shard_map/chunk_layer/pallas_call | solution.py:145
  73.6 11.0 %chunk_layer.5 = (bf16[4,128,512]{2,1,0:T(8,128)(2,1)S(1)}, bf16[4,512,64]{2,1,0:T(8,128)(2,1)S(1)}) custom-call(s32[5]{0:T(128)S(1)} %pad_add_fusion.1.scalars, bf16[4,4,128,512]{3,2,1,0:T(8,128)(2,1)S(1)} %bitcast.43, bf16[4,1,128,512]{3,2,1,0:T(8,128)(2,1)} %collective-permute-done.6.sib_ref, bf16[4,1,128,512]{3,2,1,0:T(8,128)(2,1)} %collective-permute-done.7.far_ref, ...), custom_call_target="tpu_custom_call" | custom-call | flops 5368709120 | bytes 12582912 | tf_op jit(solution)/shard_map/chunk_layer/pallas_call | solution.py:145
  85.3 10.7 %chunk_layer.6 = (bf16[4,128,512]{2,1,0:T(8,128)(2,1)S(1)}, bf16[4,512,64]{2,1,0:T(8,128)(2,1)S(1)}) custom-call(s32[5]{0:T(128)S(1)} %pad_add_fusion.2.scalars, bf16[4,4,128,512]{3,2,1,0:T(8,128)(2,1)S(1)} %bitcast.44, bf16[4,1,128,512]{3,2,1,0:T(8,128)(2,1)S(1)} %collective-permute-done.9.sib_ref, ...), custom_call_target="tpu_custom_call" | custom-call | flops 5368709120 | bytes 12582912 | tf_op jit(solution)/shard_map/chunk_layer/pallas_call | solution.py:145
  96.9 10.4 %chunk_layer.7 = (bf16[4,128,512]{2,1,0:T(8,128)(2,1)S(1)}, bf16[4,512,64]{2,1,0:T(8,128)(2,1)S(1)}) custom-call(s32[5]{0:T(128)S(1)} %pad_add_fusion.3.scalars, bf16[4,4,128,512]{3,2,1,0:T(8,128)(2,1)S(1)} %bitcast.45, bf16[4,1,128,512]{3,2,1,0:T(8,128)(2,1)S(1)} %collective-permute-done.12.sib_ref, ...), custom_call_target="tpu_custom_call" | custom-call | flops 5368709120 | bytes 12582912 | tf_op jit(solution)/shard_map/chunk_layer/pallas_call | solution.py:145
  108.1 1.8 %pad_maximum_fusion = bf16[16,512,64]{2,1,0:T(8,128)(2,1)} fusion(bf16[4,512,64]{2,1,0:T(8,128)(2,1)S(1)} %get-tuple-element.17, bf16[4,512,64]{2,1,0:T(8,128)(2,1)S(1)} %get-tuple-element.16, bf16[4,512,64]{2,1,0:T(8,128)(2,1)S(1)} %get-tuple-element.15, bf16[4,512,64]{2,1,0:T(8,128)(2,1)S(1)} %get-tuple-element.14), kind=kLoop, calls=%fused_computation.46 | loop fusion | flops 1572864 | bytes 2097152 | tf_op jit(solution)/shard_map/concatenate | solution.py:307
  110.0 3.2 %reshape.145 = bf16[16,32768]{1,0:T(8,128)(2,1)S(1)} reshape(bf16[16,512,64]{2,1,0:T(8,128)(2,1)} %pad_maximum_fusion) | data formatting | bytes 2097152 | tf_op jit(solution)/shard_map/reshape | solution.py:307
  115.1 1.5 convolution_convert_fusion.1
  119.0 1.1 collective-permute-done.19
  121.1 1.6 collective-permute-start.17
  123.2 2.4 %collective-permute-done.20 = bf16[128,512]{1,0:T(8,128)(2,1)S(1)} collective-permute-done((bf16[128,512]{1,0:T(8,128)(2,1)S(1)}, bf16[128,512]{1,0:T(8,128)(2,1)S(1)}, u32[]{:S(2)}, u32[]{:S(2)}) %collective-permute-start.20) | collective-permute-done | bytes 131104 | tf_op jit(solution)/shard_map/ppermute | solution.py:214
  126.8 1.6 collective-permute-start.29
  128.9 2.6 %collective-permute-done.21 = bf16[128,512]{1,0:T(8,128)(2,1)} collective-permute-done((bf16[128,512]{1,0:T(8,128)(2,1)S(1)}, bf16[128,512]{1,0:T(8,128)(2,1)}, u32[]{:S(2)}, u32[]{:S(2)}) %collective-permute-start.21) | collective-permute-done | bytes 131104 | tf_op jit(solution)/shard_map/ppermute | solution.py:214
  131.4 1.0 collective-permute-done.25
  133.0 4.1 %collective-permute-done.30 = bf16[4,32768]{1,0:T(4,128)(2,1)S(1)} collective-permute-done((bf16[4,32768]{1,0:T(4,128)(2,1)S(1)}, bf16[4,32768]{1,0:T(4,128)(2,1)S(1)}, u32[]{:S(2)}, u32[]{:S(2)}) %collective-permute-start.30) | collective-permute-done | bytes 262176 | tf_op jit(solution)/shard_map/ppermute | solution.py:314
  137.1 16.7 %collective-permute-done.31 = bf16[4,32768]{1,0:T(4,128)(2,1)S(1)} collective-permute-done((bf16[4,32768]{1,0:T(4,128)(2,1)S(1)}, bf16[4,32768]{1,0:T(4,128)(2,1)S(1)}, u32[]{:S(2)}, u32[]{:S(2)}) %collective-permute-start.31) | collective-permute-done | bytes 262176 | tf_op jit(solution)/shard_map/ppermute | solution.py:314
  154.3 1.7 convolution_convert_fusion
  156.0 3.7 %collective-permute-done.22 = bf16[128,512]{1,0:T(8,128)(2,1)S(1)} collective-permute-done((bf16[128,512]{1,0:T(8,128)(2,1)S(1)}, bf16[128,512]{1,0:T(8,128)(2,1)S(1)}, u32[]{:S(2)}, u32[]{:S(2)}) %collective-permute-start.22) | collective-permute-done | bytes 131104 | tf_op jit(solution)/shard_map/ppermute | solution.py:214
  159.8 9.6 %fusion.8 = bf16[512,2048]{1,0:T(8,128)(2,1)} fusion(bf16[512,2048]{1,0:T(8,128)(2,1)} %collective-permute-done.29, bf16[512,2048]{1,0:T(8,128)(2,1)} %all-gather.2.cloned.1.call-done, bf16[512,2048]{1,0:T(8,128)(2,1)} %collective-permute-done.27, bf16[512,2048]{1,0:T(8,128)(2,1)} %param.20, bf16[128,512]{1,0:T(8,128)(2,1)S(1)} %collective-permute-done.26, ...), kind=kOutput, calls=%fused_computation.14 | convolution fusion | flops 4363124736 | bytes 12582912 | tf_op jit(solution)/shard_map/dot_general | solution.py:322
  (146 shorter events, 20.2 us)
Async XLA Ops:
  7.2 119.7 %all-gather.2.cloned.1.call-start = ((), (), s32[]{:S(2)}) async-start(), calls=%async_computation | async-start | bytes 2359296 | tf_op jit(solution)/shard_map/all_gather | solution.py:276
  10.2 29.2 %collective-permute-start.1 = (bf16[4,1,128,512]{3,2,1,0:T(8,128)(2,1)}, bf16[4,1,128,512]{3,2,1,0:T(8,128)(2,1)}, u32[]{:S(2)}, u32[]{:S(2)}) collective-permute-start(bf16[4,1,128,512]{3,2,1,0:T(8,128)(2,1)} %get-tuple-element.20), channel_id=1, source_target_pairs={{0,2},{1,3},{2,0},{3,1},{4,6},{5,7},{6,4},{7,5},{8,10},{9,11},{10,... | collective-permute-start | bytes 1572872 | tf_op jit(solution)/shard_map/ppermute | solution.py:214
  13.1 37.5 %collective-permute-start = (bf16[4,1,128,512]{3,2,1,0:T(8,128)(2,1)}, bf16[4,1,128,512]{3,2,1,0:T(8,128)(2,1)S(1)}, u32[]{:S(2)}, u32[]{:S(2)}) collective-permute-start(bf16[4,1,128,512]{3,2,1,0:T(8,128)(2,1)} %get-tuple-element.20), channel_id=1, source_target_pairs={{0,1},{1,0},{2,3},{3,2},{4,5},{5,4},{6,7},{7,6},{8,9},{9,8},{10,11... | collective-permute-start | bytes 1572872 | tf_op jit(solution)/shard_map/ppermute | solution.py:214
  15.3 11.1 %collective-permute-start.3 = (bf16[4,32768]{1,0:T(4,128)(2,1)S(1)}, bf16[4,32768]{1,0:T(4,128)(2,1)}, u32[]{:S(2)}, u32[]{:S(2)}) collective-permute-start(bf16[4,32768]{1,0:T(4,128)(2,1)S(1)} %get-tuple-element.31), channel_id=1, source_target_pairs={{0,4},{4,8},{8,12},{12,0},{1,5},{5,9},{9,13},{13,1},{2,6},{6,10},{... | collective-permute-start | bytes 786440 | tf_op jit(solution)/shard_map/ppermute | solution.py:220
  16.8 20.3 %collective-permute-start.4 = (bf16[4,32768]{1,0:T(4,128)(2,1)S(1)}, bf16[4,32768]{1,0:T(4,128)(2,1)}, u32[]{:S(2)}, u32[]{:S(2)}) collective-permute-start(bf16[4,32768]{1,0:T(4,128)(2,1)S(1)} %get-tuple-element.30), channel_id=1, source_target_pairs={{0,8},{4,12},{8,0},{12,4},{1,9},{5,13},{9,1},{13,5},{2,10},{6,14},... | collective-permute-start | bytes 786440 | tf_op jit(solution)/shard_map/ppermute | solution.py:220
  20.4 18.4 %collective-permute-start.28 = (bf16[64,2048]{1,0:T(8,128)(2,1)S(1)}, bf16[64,2048]{1,0:T(8,128)(2,1)S(1)}, u32[]{:S(2)}, u32[]{:S(2)}) collective-permute-start(bf16[64,2048]{1,0:T(8,128)(2,1)S(1)} %constant_dynamic-slice_fusion), channel_id=1, source_target_pairs={{0,2},{1,3},{2,0},{3,1},{4,6},{5,7},{6,4},{7,5},{8,10},{9,11},{10,... | collective-permute-start | bytes 786440 | tf_op jit(solution)/shard_map/ppermute | solution.py:214
  26.3 26.6 %collective-permute-start.7 = (bf16[4,1,128,512]{3,2,1,0:T(8,128)(2,1)}, bf16[4,1,128,512]{3,2,1,0:T(8,128)(2,1)}, u32[]{:S(2)}, u32[]{:S(2)}) collective-permute-start(bf16[4,1,128,512]{3,2,1,0:T(8,128)(2,1)} %get-tuple-element.23), channel_id=1, source_target_pairs={{0,2},{1,3},{2,0},{3,1},{4,6},{5,7},{6,4},{7,5},{8,10},{9,11},{10,... | collective-permute-start | bytes 1572872 | tf_op jit(solution)/shard_map/ppermute | solution.py:214
  37.2 12.9 %collective-permute-start.5 = (bf16[4,32768]{1,0:T(4,128)(2,1)}, bf16[4,32768]{1,0:T(4,128)(2,1)}, u32[]{:S(2)}, u32[]{:S(2)}) collective-permute-start(bf16[4,32768]{1,0:T(4,128)(2,1)} %get-tuple-element.29), channel_id=1, source_target_pairs={{0,12},{4,0},{8,4},{12,8},{1,13},{5,1},{9,5},{13,9},{2,14},{6,2},{... | collective-permute-start | bytes 786440 | tf_op jit(solution)/shard_map/ppermute | solution.py:220
  38.8 21.2 %collective-permute-start.10 = (bf16[4,1,128,512]{3,2,1,0:T(8,128)(2,1)}, bf16[4,1,128,512]{3,2,1,0:T(8,128)(2,1)}, u32[]{:S(2)}, u32[]{:S(2)}) collective-permute-start(bf16[4,1,128,512]{3,2,1,0:T(8,128)(2,1)} %get-tuple-element.22), channel_id=1, source_target_pairs={{0,2},{1,3},{2,0},{3,1},{4,6},{5,7},{6,4},{7,5},{8,10},{9,11},{10,... | collective-permute-start | bytes 1572872 | tf_op jit(solution)/shard_map/ppermute | solution.py:214
  39.3 21.2 %collective-permute-start.2 = (bf16[4,1,128,512]{3,2,1,0:T(8,128)(2,1)}, bf16[4,1,128,512]{3,2,1,0:T(8,128)(2,1)}, u32[]{:S(2)}, u32[]{:S(2)}) collective-permute-start(bf16[4,1,128,512]{3,2,1,0:T(8,128)(2,1)} %collective-permute-done.1.far_ref), channel_id=1, source_target_pairs={{0,1},{1,0},{2,3},{3,2},{4,5},{5,4},{6,7},{7,6},{8,9},{9,8},{10,11... | collective-permute-start | bytes 1572872 | tf_op jit(solution)/shard_map/ppermute | solution.py:214
  50.1 22.9 %collective-permute-start.6 = (bf16[4,1,128,512]{3,2,1,0:T(8,128)(2,1)}, bf16[4,1,128,512]{3,2,1,0:T(8,128)(2,1)}, u32[]{:S(2)}, u32[]{:S(2)}) collective-permute-start(bf16[4,1,128,512]{3,2,1,0:T(8,128)(2,1)} %get-tuple-element.23), channel_id=1, source_target_pairs={{0,1},{1,0},{2,3},{3,2},{4,5},{5,4},{6,7},{7,6},{8,9},{9,8},{10,11... | collective-permute-start | bytes 1572872 | tf_op jit(solution)/shard_map/ppermute | solution.py:214
  51.4 22.1 %collective-permute-start.13 = (bf16[4,1,128,512]{3,2,1,0:T(8,128)(2,1)}, bf16[4,1,128,512]{3,2,1,0:T(8,128)(2,1)}, u32[]{:S(2)}, u32[]{:S(2)}) collective-permute-start(bf16[4,1,128,512]{3,2,1,0:T(8,128)(2,1)} %get-tuple-element.21), channel_id=1, source_target_pairs={{0,2},{1,3},{2,0},{3,1},{4,6},{5,7},{6,4},{7,5},{8,10},{9,11},{10,... | collective-permute-start | bytes 1572872 | tf_op jit(solution)/shard_map/ppermute | solution.py:214
  52.9 20.7 %collective-permute-start.8 = (bf16[4,1,128,512]{3,2,1,0:T(8,128)(2,1)}, bf16[4,1,128,512]{3,2,1,0:T(8,128)(2,1)}, u32[]{:S(2)}, u32[]{:S(2)}) collective-permute-start(bf16[4,1,128,512]{3,2,1,0:T(8,128)(2,1)} %collective-permute-done.7.far_ref), channel_id=1, source_target_pairs={{0,1},{1,0},{2,3},{3,2},{4,5},{5,4},{6,7},{7,6},{8,9},{9,8},{10,11... | collective-permute-start | bytes 1572872 | tf_op jit(solution)/shard_map/ppermute | solution.py:214
  60.0 25.3 %collective-permute-start.9 = (bf16[4,1,128,512]{3,2,1,0:T(8,128)(2,1)}, bf16[4,1,128,512]{3,2,1,0:T(8,128)(2,1)S(1)}, u32[]{:S(2)}, u32[]{:S(2)}) collective-permute-start(bf16[4,1,128,512]{3,2,1,0:T(8,128)(2,1)} %get-tuple-element.22), channel_id=1, source_target_pairs={{0,1},{1,0},{2,3},{3,2},{4,5},{5,4},{6,7},{7,6},{8,9},{9,8},{10,11... | collective-permute-start | bytes 1572872 | tf_op jit(solution)/shard_map/ppermute | solution.py:214
  60.5 24.8 %collective-permute-start.11 = (bf16[4,1,128,512]{3,2,1,0:T(8,128)(2,1)}, bf16[4,1,128,512]{3,2,1,0:T(8,128)(2,1)S(1)}, u32[]{:S(2)}, u32[]{:S(2)}) collective-permute-start(bf16[4,1,128,512]{3,2,1,0:T(8,128)(2,1)} %collective-permute-done.10.far_ref), channel_id=1, source_target_pairs={{0,1},{1,0},{2,3},{3,2},{4,5},{5,4},{6,7},{7,6},{8,9},{9,8},{10,11... | collective-permute-start | bytes 1572872 | tf_op jit(solution)/shard_map/ppermute | solution.py:214
  73.1 23.8 %collective-permute-start.12 = (bf16[4,1,128,512]{3,2,1,0:T(8,128)(2,1)S(1)}, bf16[4,1,128,512]{3,2,1,0:T(8,128)(2,1)S(1)}, u32[]{:S(2)}, u32[]{:S(2)}) collective-permute-start(bf16[4,1,128,512]{3,2,1,0:T(8,128)(2,1)S(1)} %copy-done.16), channel_id=1, source_target_pairs={{0,1},{1,0},{2,3},{3,2},{4,5},{5,4},{6,7},{7,6},{8,9},{9,8},{10,11... | collective-permute-start | bytes 1572872 | tf_op jit(solution)/shard_map/ppermute | solution.py:214
  73.5 23.4 %collective-permute-start.14 = (bf16[4,1,128,512]{3,2,1,0:T(8,128)(2,1)}, bf16[4,1,128,512]{3,2,1,0:T(8,128)(2,1)S(1)}, u32[]{:S(2)}, u32[]{:S(2)}) collective-permute-start(bf16[4,1,128,512]{3,2,1,0:T(8,128)(2,1)} %collective-permute-done.13.far_ref), channel_id=1, source_target_pairs={{0,1},{1,0},{2,3},{3,2},{4,5},{5,4},{6,7},{7,6},{8,9},{9,8},{10,11... | collective-permute-start | bytes 1572872 | tf_op jit(solution)/shard_map/ppermute | solution.py:214
  113.7 6.4 %collective-permute-start.19 = (bf16[128,512]{1,0:T(8,128)(2,1)S(1)}, bf16[128,512]{1,0:T(8,128)(2,1)S(1)}, u32[]{:S(2)}, u32[]{:S(2)}) collective-permute-start(bf16[128,512]{1,0:T(8,128)(2,1)S(1)} %get-tuple-element.34), channel_id=1, source_target_pairs={{0,2},{1,3},{2,0},{3,1},{4,6},{5,7},{6,4},{7,5},{8,10},{9,11},{10,... | collective-permute-start | bytes 393224 | tf_op jit(solution)/shard_map/ppermute | solution.py:214
  114.3 6.9 %collective-permute-start.23 = (bf16[128,512]{1,0:T(8,128)(2,1)S(1)}, bf16[128,512]{1,0:T(8,128)(2,1)S(1)}, u32[]{:S(2)}, u32[]{:S(2)}) collective-permute-start(bf16[128,512]{1,0:T(8,128)(2,1)S(1)} %get-tuple-element.33), channel_id=1, source_target_pairs={{0,3},{1,2},{2,1},{3,0},{4,7},{5,6},{6,5},{7,4},{8,11},{9,10},{10,... | collective-permute-start | bytes 393224 | tf_op jit(solution)/shard_map/ppermute | solution.py:214
  116.7 6.0 %collective-permute-start.16 = (bf16[128,512]{1,0:T(8,128)(2,1)S(1)}, bf16[128,512]{1,0:T(8,128)(2,1)S(1)}, u32[]{:S(2)}, u32[]{:S(2)}) collective-permute-start(bf16[128,512]{1,0:T(8,128)(2,1)S(1)} %get-tuple-element.39), channel_id=1, source_target_pairs={{0,1},{1,0},{2,3},{3,2},{4,5},{5,4},{6,7},{7,6},{8,9},{9,8},{10,11... | collective-permute-start | bytes 393224 | tf_op jit(solution)/shard_map/ppermute | solution.py:214
  117.5 8.2 %collective-permute-start.20 = (bf16[128,512]{1,0:T(8,128)(2,1)S(1)}, bf16[128,512]{1,0:T(8,128)(2,1)S(1)}, u32[]{:S(2)}, u32[]{:S(2)}) collective-permute-start(bf16[128,512]{1,0:T(8,128)(2,1)S(1)} %get-tuple-element.38), channel_id=1, source_target_pairs={{0,2},{1,3},{2,0},{3,1},{4,6},{5,7},{6,4},{7,5},{8,10},{9,11},{10,... | collective-permute-start | bytes 393224 | tf_op jit(solution)/shard_map/ppermute | solution.py:214
  118.0 8.8 %collective-permute-start.24 = (bf16[128,512]{1,0:T(8,128)(2,1)S(1)}, bf16[128,512]{1,0:T(8,128)(2,1)}, u32[]{:S(2)}, u32[]{:S(2)}) collective-permute-start(bf16[128,512]{1,0:T(8,128)(2,1)S(1)} %get-tuple-element.37), channel_id=1, source_target_pairs={{0,3},{1,2},{2,1},{3,0},{4,7},{5,6},{6,5},{7,4},{8,11},{9,10},{10,... | collective-permute-start | bytes 393224 | tf_op jit(solution)/shard_map/ppermute | solution.py:214
  120.1 39.7 %collective-permute-start.27 = (bf16[512,2048]{1,0:T(8,128)(2,1)}, bf16[512,2048]{1,0:T(8,128)(2,1)}, u32[]{:S(2)}, u32[]{:S(2)}) collective-permute-start(bf16[512,2048]{1,0:T(8,128)(2,1)} %param.20), channel_id=1, source_target_pairs={{0,1},{1,0},{2,3},{3,2},{4,5},{5,4},{6,7},{7,6},{8,9},{9,8},{10,11... | collective-permute-start | bytes 6291464 | tf_op jit(solution)/shard_map/ppermute | solution.py:214
  121.1 7.7 %collective-permute-start.17 = (bf16[128,512]{1,0:T(8,128)(2,1)S(1)}, bf16[128,512]{1,0:T(8,128)(2,1)}, u32[]{:S(2)}, u32[]{:S(2)}) collective-permute-start(bf16[128,512]{1,0:T(8,128)(2,1)S(1)} %get-tuple-element.43), channel_id=1, source_target_pairs={{0,1},{1,0},{2,3},{3,2},{4,5},{5,4},{6,7},{7,6},{8,9},{9,8},{10,11... | collective-permute-start | bytes 393224 | tf_op jit(solution)/shard_map/ppermute | solution.py:214
  122.7 8.7 %collective-permute-start.21 = (bf16[128,512]{1,0:T(8,128)(2,1)S(1)}, bf16[128,512]{1,0:T(8,128)(2,1)}, u32[]{:S(2)}, u32[]{:S(2)}) collective-permute-start(bf16[128,512]{1,0:T(8,128)(2,1)S(1)} %get-tuple-element.42), channel_id=1, source_target_pairs={{0,2},{1,3},{2,0},{3,1},{4,6},{5,7},{6,4},{7,5},{8,10},{9,11},{10,... | collective-permute-start | bytes 393224 | tf_op jit(solution)/shard_map/ppermute | solution.py:214
  125.7 6.8 %collective-permute-start.25 = (bf16[128,512]{1,0:T(8,128)(2,1)S(1)}, bf16[128,512]{1,0:T(8,128)(2,1)}, u32[]{:S(2)}, u32[]{:S(2)}) collective-permute-start(bf16[128,512]{1,0:T(8,128)(2,1)S(1)} %get-tuple-element.41), channel_id=1, source_target_pairs={{0,3},{1,2},{2,1},{3,0},{4,7},{5,6},{6,5},{7,4},{8,11},{9,10},{10,... | collective-permute-start | bytes 393224 | tf_op jit(solution)/shard_map/ppermute | solution.py:214
  126.8 32.9 %collective-permute-start.29 = (bf16[512,2048]{1,0:T(8,128)(2,1)}, bf16[512,2048]{1,0:T(8,128)(2,1)}, u32[]{:S(2)}, u32[]{:S(2)}) collective-permute-start(bf16[512,2048]{1,0:T(8,128)(2,1)} %all-gather.2.cloned.1.call-done), channel_id=1, source_target_pairs={{0,1},{1,0},{2,3},{3,2},{4,5},{5,4},{6,7},{7,6},{8,9},{9,8},{10,11... | collective-permute-start | bytes 6291464 | tf_op jit(solution)/shard_map/ppermute | solution.py:214
  128.8 8.3 %collective-permute-start.30 = (bf16[4,32768]{1,0:T(4,128)(2,1)S(1)}, bf16[4,32768]{1,0:T(4,128)(2,1)S(1)}, u32[]{:S(2)}, u32[]{:S(2)}) collective-permute-start(bf16[4,32768]{1,0:T(4,128)(2,1)S(1)} %get-tuple-element.27), channel_id=1, source_target_pairs={{0,12},{4,0},{8,4},{12,8},{1,13},{5,1},{9,5},{13,9},{2,14},{6,2},{... | collective-permute-start | bytes 786440 | tf_op jit(solution)/shard_map/ppermute | solution.py:314
  131.4 22.3 %collective-permute-start.31 = (bf16[4,32768]{1,0:T(4,128)(2,1)S(1)}, bf16[4,32768]{1,0:T(4,128)(2,1)S(1)}, u32[]{:S(2)}, u32[]{:S(2)}) collective-permute-start(bf16[4,32768]{1,0:T(4,128)(2,1)S(1)} %get-tuple-element.26), channel_id=1, source_target_pairs={{0,8},{4,12},{8,0},{12,4},{1,9},{5,13},{9,1},{13,5},{2,10},{6,14},... | collective-permute-start | bytes 786440 | tf_op jit(solution)/shard_map/ppermute | solution.py:314
  132.5 21.4 %collective-permute-start.32 = (bf16[4,32768]{1,0:T(4,128)(2,1)S(1)}, bf16[4,32768]{1,0:T(4,128)(2,1)S(1)}, u32[]{:S(2)}, u32[]{:S(2)}) collective-permute-start(bf16[4,32768]{1,0:T(4,128)(2,1)S(1)} %get-tuple-element.25), channel_id=1, source_target_pairs={{0,4},{4,8},{8,12},{12,0},{1,5},{5,9},{9,13},{13,1},{2,6},{6,10},{... | collective-permute-start | bytes 786440 | tf_op jit(solution)/shard_map/ppermute | solution.py:314
  137.1 19.0 %collective-permute-start.18 = (bf16[128,512]{1,0:T(8,128)(2,1)S(1)}, bf16[128,512]{1,0:T(8,128)(2,1)S(1)}, u32[]{:S(2)}, u32[]{:S(2)}) collective-permute-start(bf16[128,512]{1,0:T(8,128)(2,1)S(1)} %get-tuple-element.47), channel_id=1, source_target_pairs={{0,1},{1,0},{2,3},{3,2},{4,5},{5,4},{6,7},{7,6},{8,9},{9,8},{10,11... | collective-permute-start | bytes 393224 | tf_op jit(solution)/shard_map/ppermute | solution.py:214
  153.8 6.0 %collective-permute-start.22 = (bf16[128,512]{1,0:T(8,128)(2,1)S(1)}, bf16[128,512]{1,0:T(8,128)(2,1)S(1)}, u32[]{:S(2)}, u32[]{:S(2)}) collective-permute-start(bf16[128,512]{1,0:T(8,128)(2,1)S(1)} %get-tuple-element.46), channel_id=1, source_target_pairs={{0,2},{1,3},{2,0},{3,1},{4,6},{5,7},{6,4},{7,5},{8,10},{9,11},{10,... | collective-permute-start | bytes 393224 | tf_op jit(solution)/shard_map/ppermute | solution.py:214
  (34 other events, 331.6 us)
Sparse Core Ops, SparseCore 0:
  50.1 47.7 all-gather.1

commit v2 on v1

v2 whole, which is shorter than its diff:
```python
import functools

import jax
import jax.numpy as jnp
from jax import lax
from jax.experimental import pallas as pl
from jax.experimental.pallas import tpu as pltpu
from jax.sharding import PartitionSpec as P

F32 = jnp.float32
BF16 = jnp.bfloat16


def rank_within(keys, order):
    earlier = (keys[None, :] == keys[:, None]) & (order[None, :] < order[:, None])
    return jnp.sum(earlier.astype(jnp.int32), axis=1)


def one_hot_rows(wanted, count):
    places = jnp.arange(count, dtype=jnp.int32)
    return (wanted[:, None] == places[None, :]).astype(BF16)


def xor_place(me, mask):
    return lax.rem(lax.rem(me, 2) + mask % 2, 2) + 2 * lax.rem(me // 2 + mask // 2, 2)


def layer_kernel(
    heads,
    head_size,
    state_size,
    chunks,
    parts,
    shards,
    scalars,
    tokens_ref,
    outbound_ref,
    x_ref,
    z_ref,
    bd_ref,
    bias_ref,
    rate_ref,
    gain_ref,
    mixed_ref,
    state_ref,
    own,
    sib,
    far,
    diag,
    inbound,
    acc_ref,
    normed_ref,
    own_sem,
    sib_send,
    sib_recv,
    far_send,
    far_recv,
    diag_send,
    diag_recv,
    store_send,
    store_recv,
    store_local,
    norm_send,
    norm_recv,
    norm_local,
):
    slots = tokens_ref.shape[2]
    depth = tokens_ref.shape[3]
    inner = heads * head_size
    capacity = outbound_ref.shape[1]
    me = lax.axis_index("mp")
    dp = lax.axis_index("dp")
    MESH = pl.DeviceIdType.MESH

    barrier = pltpu.get_barrier_semaphore()
    for mask in range(1, parts):
        pl.semaphore_signal(
            barrier, inc=1, device_id={"mp": xor_place(me, mask)}, device_id_type=MESH
        )
    for k in range(1, shards):
        pl.semaphore_signal(
            barrier, inc=1, device_id={"dp": lax.rem(dp + k, shards)}, device_id_type=MESH
        )
    pl.semaphore_wait(barrier, parts - 1 + shards - 1)

    def remote(src, dst, send, recv, device):
        return pltpu.make_async_remote_copy(
            src_ref=src,
            dst_ref=dst,
            send_sem=send,
            recv_sem=recv,
            device_id=device,
            device_id_type=MESH,
        )

    def far_copy(j):
        return remote(
            tokens_ref.at[:, j], far.at[j], far_send.at[j], far_recv.at[j], {"mp": xor_place(me, 2)}
        )

    def sib_copy(j):
        return remote(
            tokens_ref.at[:, j], sib.at[j], sib_send.at[j], sib_recv.at[j], {"mp": xor_place(me, 1)}
        )

    def diag_copy(j):
        return remote(
            far.at[j], diag.at[j], diag_send.at[j], diag_recv.at[j], {"mp": xor_place(me, 1)}
        )

    def own_copy(j):
        return pltpu.make_async_copy(tokens_ref.at[:, j], own.at[j], own_sem.at[j])

    def store_copy(k):
        return remote(
            outbound_ref.at[k],
            inbound.at[k],
            store_send.at[k],
            store_recv.at[k],
            {"dp": lax.rem(dp + k, shards)},
        )

    store_here = pltpu.make_async_copy(outbound_ref.at[0], inbound.at[0], store_local)

    def norm_target(j, k):
        return mixed_ref.at[pl.ds(pl.multiple_of(j * slots, slots), slots), k * inner : (k + 1) * inner]

    def norm_copy(j, k):
        return remote(
            normed_ref.at[j, k],
            norm_target(j, k),
            norm_send.at[j, k],
            norm_recv.at[j, k],
            {"mp": xor_place(me, k)},
        )

    def norm_here(j):
        return pltpu.make_async_copy(normed_ref.at[j, 0], norm_target(j, 0), norm_local.at[j])

    ahead = min(2, chunks)
    for j in range(ahead):
        far_copy(j).start()
    for k in range(1, shards):
        store_copy(k).start()
    store_here.start()
    for j in range(chunks):
        own_copy(j).start()
        sib_copy(j).start()

    lane = lax.broadcasted_iota(jnp.int32, (slots, slots), 1)
    row = lax.broadcasted_iota(jnp.int32, (slots, slots), 0)
    causal = row >= lane
    low = lane < head_size
    lane8 = lax.broadcasted_iota(jnp.int32, (heads, slots), 1)
    pair = 2 * head_size

    def session(j, step):
        place = lax.rem(lax.rem(me, 2) + lax.rem(step, 2), 2) + 2 * lax.rem(me // 2 + step // 2, 2)
        here = pl.ds(pl.multiple_of(place * slots, slots), slots)
        index = j * parts + step
        count = scalars[index]
        spot = scalars[chunks * parts + index]
        spot_k = spot // capacity
        spot_c = spot - spot_k * capacity
        slab = acc_ref[here, 2 * inner : 2 * inner + 128]
        b_bf = slab[:, :state_size].astype(BF16)
        b_f32 = b_bf.astype(F32)
        c_bf = acc_ref[here, 2 * inner + 128 : 2 * inner + 128 + state_size].astype(BF16)
        raw = slab.T[state_size : state_size + heads, :] + bias_ref[...]
        dt_t = jnp.maximum(raw, 0.0) + jnp.log1p(jnp.exp(-jnp.abs(raw)))
        dt_t = jnp.where(lane8 < count, dt_t, 0.0)
        cum_t = dt_t * rate_ref[...]
        shift = 1
        while shift < slots:
            moved = pltpu.roll(cum_t, shift, axis=1)
            cum_t = cum_t + jnp.where(lane8 >= shift, moved, 0.0)
            shift *= 2
        last = cum_t[:, slots - 1 : slots]
        weigh_t = jnp.exp(cum_t - last) * dt_t
        fade_t = jnp.exp(-cum_t)
        stacked = jnp.concatenate(
            [cum_t, weigh_t, fade_t, jnp.zeros((slots - 3 * heads, slots), F32)], axis=0
        ).T
        scores = lax.dot_general(
            c_bf, b_bf, (((1,), (1,)), ((), ())), preferred_element_type=F32
        )
        gated_parts = []
        squares = None
        for g in range(heads // 2):
            cols = slice(g * pair, (g + 1) * pair)
            xs = acc_ref[here, cols].astype(BF16)
            zs = acc_ref[here, inner + g * pair : inner + (g + 1) * pair].astype(BF16).astype(F32)
            split = jnp.concatenate(
                [jnp.where(low, xs, jnp.zeros((), BF16)), jnp.where(low, jnp.zeros((), BF16), xs)],
                axis=0,
            )
            mixes = []
            weighed = []
            for h in (2 * g, 2 * g + 1):
                gaps = jnp.where(causal, cum_t[h : h + 1, :] - stacked[:, h : h + 1], -1e30)
                mixes.append((jnp.exp(gaps) * dt_t[h : h + 1, :] * scores).astype(BF16))
                weighed.append((b_f32 * stacked[:, heads + h : heads + h + 1]).astype(BF16))
            y = jnp.dot(jnp.concatenate(mixes, axis=1), split, preferred_element_type=F32)
            start = inbound[spot_k, spot_c, cols, :]
            carried = lax.dot_general(
                c_bf, start, (((1,), (1,)), ((), ())), preferred_element_type=F32
            )
            fade0 = stacked[:, 2 * heads + 2 * g : 2 * heads + 2 * g + 1]
            fade1 = stacked[:, 2 * heads + 2 * g + 1 : 2 * heads + 2 * g + 2]
            y = y + carried * jnp.where(low, fade0, fade1)
            grown = lax.dot_general(
                split,
                jnp.concatenate(weighed, axis=0),
                (((0,), (0,)), ((), ())),
                preferred_element_type=F32,
            )
            keep = jnp.where(
                row[:, :state_size] < head_size,
                fade_t[2 * g : 2 * g + 1, slots - 1 : slots],
                fade_t[2 * g + 1 : 2 * g + 2, slots - 1 : slots],
            )
            state_ref[index, cols, :] = (keep * start.astype(F32) + grown).astype(BF16)
            gated = y * (zs * jax.nn.sigmoid(zs))
            part = jnp.sum(gated * gated, axis=1, keepdims=True)
            squares = part if squares is None else squares + part
            gated_parts.append(gated)
        scale = lax.rsqrt(squares * (1.0 / inner) + 1e-05)
        scale = jnp.where(row[:, :1] < count, scale, 0.0)
        for g in range(heads // 2):
            cols = slice(g * pair, (g + 1) * pair)
            normed_ref[j, step, :, cols] = (gated_parts[g] * scale * gain_ref[:, cols]).astype(BF16)

    def compute(j):
        own_copy(j).wait()
        sib_copy(j).wait_recv()
        diag_copy(j).wait_recv()
        pieces = []
        for step, ref in enumerate((own, sib, far, diag)):
            rows = pl.ds(pl.multiple_of(xor_place(me, step) * depth, depth), depth)
            pieces.append((ref[j].reshape(parts * slots, depth), rows))
        base = 0
        for weight in (x_ref, z_ref, bd_ref):
            width = weight.shape[1]
            total = None
            for values, rows in pieces:
                piece = jnp.dot(values, weight[rows, :], preferred_element_type=F32)
                total = piece if total is None else total + piece
            acc_ref[:, base : base + width] = total
            base += width

        def run_session(step, carry):
            session(j, step)
            return carry

        lax.fori_loop(0, parts, run_session, 0)
        norm_here(j).start()
        for k in range(1, parts):
            norm_copy(j, k).start()

    def round_trip(j, carry):
        @pl.when(j < chunks)
        def _():
            far_copy(j).wait_recv()
            diag_copy(j).start()

        @pl.when(j + ahead < chunks)
        def _():
            far_copy(j + ahead).start()

        @pl.when(j == 1)
        def _():
            store_here.wait()
            for k in range(1, shards):
                store_copy(k).wait_recv()

        @pl.when(j > 0)
        def _():
            compute(j - 1)

        return carry

    lax.fori_loop(0, chunks + 1, round_trip, 0)

    for j in range(chunks):
        far_copy(j).wait_send()
        sib_copy(j).wait_send()
        diag_copy(j).wait_send()
        norm_here(j).wait()
        for k in range(1, parts):
            norm_copy(j, k).wait()
    for k in range(1, shards):
        store_copy(k).wait_send()


def run_layer(scalars, tokens4, outbound, x_weight, z_weight, bd_weight, bias, rate, gain, sizes, shards):
    heads, head_size, state_size = sizes
    parts, chunks, slots, depth = tokens4.shape
    inner = heads * head_size
    width = 2 * inner + bd_weight.shape[1]
    rows = parts * slots
    capacity = outbound.shape[1]
    vmem = pl.BlockSpec(memory_space=pltpu.VMEM)
    hbm = pl.BlockSpec(memory_space=pl.ANY)
    dma = pltpu.SemaphoreType.DMA
    block = pltpu.VMEM((chunks, parts, slots, depth), BF16)
    return pl.pallas_call(
        functools.partial(layer_kernel, heads, head_size, state_size, chunks, parts, shards),
        out_shape=(
            jax.ShapeDtypeStruct((chunks * slots, parts * inner), BF16),
            jax.ShapeDtypeStruct((chunks * parts, inner, state_size), BF16),
        ),
        in_specs=[pl.BlockSpec(memory_space=pltpu.SMEM), hbm, hbm] + [vmem] * 6,
        out_specs=(hbm, vmem),
        scratch_shapes=[
            block,
            block,
            block,
            block,
            pltpu.VMEM((shards, capacity, inner, state_size), BF16),
            pltpu.VMEM((rows, width), F32),
            pltpu.VMEM((chunks, parts, slots, inner), BF16),
            dma((chunks,)),
            dma((chunks,)),
            dma((chunks,)),
            dma((chunks,)),
            dma((chunks,)),
            dma((chunks,)),
            dma((chunks,)),
            dma((shards,)),
            dma((shards,)),
            dma,
            dma((chunks, parts)),
            dma((chunks, parts)),
            dma((chunks,)),
        ],
        compiler_params=pltpu.CompilerParams(
            vmem_limit_bytes=56 * 1024 * 1024, collective_id=0, has_side_effects=True
        ),
        cost_estimate=pl.CostEstimate(
            flops=2 * chunks * rows * 4 * depth * width * 4,
            bytes_accessed=64 * 1024 * 1024,
            transcendentals=chunks * rows * heads * slots,
        ),
        name="layer",
    )(scalars, tokens4, outbound, x_weight, z_weight, bd_weight, bias, rate, gain)


def project_kernel(mixed_ref, w0_ref, w1_ref, w2_ref, w3_ref, out_ref):
    depth = w0_ref.shape[0]
    total = None
    for k, ref in enumerate((w0_ref, w1_ref, w2_ref, w3_ref)):
        piece = jnp.dot(
            mixed_ref[:, k * depth : (k + 1) * depth], ref[...], preferred_element_type=F32
        )
        total = piece if total is None else total + piece
    out_ref[...] = total.astype(out_ref.dtype)


def project(mixed, weights):
    rows, depth = mixed.shape
    width = weights[0].shape[1]
    tile = min(512, width)
    return pl.pallas_call(
        project_kernel,
        out_shape=jax.ShapeDtypeStruct((rows, width), BF16),
        grid=(width // tile,),
        in_specs=[pl.BlockSpec((rows, depth), lambda i: (0, 0))]
        + [pl.BlockSpec((weights[0].shape[0], tile), lambda i: (0, i))] * 4,
        out_specs=pl.BlockSpec((rows, tile), lambda i: (0, i)),
        compiler_params=pltpu.CompilerParams(vmem_limit_bytes=40 * 1024 * 1024),
        cost_estimate=pl.CostEstimate(
            flops=2 * rows * depth * width, bytes_accessed=12 * 1024 * 1024, transcendentals=0
        ),
        name="project",
    )(mixed, *weights)


def body(
    tokens,
    x_weight,
    z_weight,
    bc_weight,
    dt_weight,
    dt_bias,
    decay_rate,
    norm_gain,
    out_weight,
    store_states,
    home_rows,
    event_counts,
):
    shard_count = lax.axis_size("dp")
    replica_count = lax.axis_size("groups")
    parts = lax.axis_size("mp")
    me = lax.axis_index("dp")
    part = lax.axis_index("mp").astype(jnp.int32)
    sessions = store_states.shape[0]
    state_width = store_states.shape[1]
    capacity = max(2, (sessions + shard_count - 1) // shard_count)
    slot_count = shard_count * capacity
    heads = dt_bias.shape[0]
    inner = x_weight.shape[1]
    head_size = inner // heads
    state_size = bc_weight.shape[1] // 2
    model = x_weight.shape[0]
    depth = tokens.shape[1]
    slots = tokens.shape[0] // sessions
    chunks = sessions // parts

    def swap(values, mask):
        return lax.ppermute(values, "mp", [(i, i ^ mask) for i in range(parts)])

    tokens4 = tokens.reshape(parts, chunks, slots, depth)

    positions = jnp.arange(sessions, dtype=jnp.int32)
    store_rows = me * sessions + positions
    everyone = jnp.arange(home_rows.shape[0], dtype=jnp.int32)
    owner = jnp.sum(
        (home_rows[None, :] == store_rows[:, None]).astype(jnp.int32) * everyone[None, :], axis=1
    )
    server = owner // sessions
    to_server = (server - me + shard_count) % shard_count
    row_slot = to_server * capacity + rank_within(server, positions)
    back_slot = row_slot
    wanted = lax.dynamic_slice_in_dim(home_rows, me * sessions, sessions)
    home_shard = wanted // sessions
    from_home = (me - home_shard + shard_count) % shard_count
    session_slot = from_home * capacity + rank_within(home_shard, wanted % sessions)

    pack = one_hot_rows(row_slot, slot_count).T
    outbound = jnp.dot(pack, store_states, preferred_element_type=F32).astype(BF16)
    outbound = outbound.reshape(shard_count, capacity, inner, state_size)
    spots = jnp.arange(sessions, dtype=jnp.int32)
    chunk_order = jnp.bitwise_xor(spots % parts, part) * chunks + spots // parts
    pad_b = jnp.zeros((model, 128 - state_size - heads), BF16)
    pad_c = jnp.zeros((model, 128 - state_size), BF16)
    bd_weight = jnp.concatenate(
        [bc_weight[:, :state_size], dt_weight, pad_b, bc_weight[:, state_size:], pad_c], axis=1
    )
    ordered_counts = event_counts[chunk_order]

    replicas = replica_count * shard_count
    piece_rows = out_weight.shape[0] // replicas
    replica = lax.axis_index("groups") * shard_count + me
    piece = lax.dynamic_slice_in_dim(out_weight, replica * piece_rows, piece_rows, 0)
    piece = swap(piece, 2)
    far_out = lax.all_gather(piece, ("groups", "dp"), axis=0, tiled=True)
    sib_out = swap(out_weight, 1)
    diag_out = swap(far_out, 1)

    scalars = jnp.concatenate([ordered_counts, session_slot[chunk_order]])
    mixed, new_state = run_layer(
        scalars,
        tokens4,
        outbound,
        x_weight,
        z_weight,
        bd_weight,
        dt_bias[:, None],
        decay_rate[:, None],
        norm_gain[None, :],
        (heads, head_size, state_size),
        shard_count,
    )
    new_state = new_state.reshape(sessions, state_width)
    slot_of = one_hot_rows(session_slot[chunk_order], slot_count).T
    outgoing = jnp.dot(slot_of, new_state, preferred_element_type=F32).astype(BF16)
    back = [outgoing[k * capacity : (k + 1) * capacity] for k in range(shard_count)]
    arrived = [back[0]]
    for k in range(1, shard_count):
        perm = [(i, (i - k) % shard_count) for i in range(shard_count)]
        arrived.append(lax.ppermute(back[k], "dp", perm))
    returned = jnp.concatenate(arrived, axis=0)
    new_store = jnp.dot(
        one_hot_rows(back_slot, slot_count), returned, preferred_element_type=F32
    ).astype(BF16)

    out_sum = project(mixed, (out_weight, sib_out, far_out, diag_out))
    return (out_sum, new_store)


def solution(mesh):
    return jax.shard_map(
        body,
        mesh=mesh,
        in_specs=(
            P(("groups", "dp"), "mp"),
            P(None, "mp"),
            P(None, "mp"),
            P(None, "mp"),
            P(None, "mp"),
            P("mp"),
            P("mp"),
            P("mp"),
            P("mp", None),
            P(("groups", "dp"), "mp"),
            P("groups"),
            P(("groups", "dp")),
        ),
        out_specs=(P(("groups", "dp", "mp"), None), P(("groups", "dp"), "mp")),
        check_vma=False,
    )
```

time: 177 us -> 197 us (1.11)
  the two profiles are of different devices: /device:TPU:0 before, /device:TPU:11 now
where the time goes in v2:
time: 197 us
  Pallas kernels  118 us (60%)
  local copies, waits for them, and re-layouts  27 us (14%)
  waiting for transfers between devices  22.2 us (11%)
  between operations  14.1 us (7%)
  starting transfers between devices  6.89 us (3%)
  matrix products  6.01 us (3%)
  other arithmetic  2.68 us (1%)
    pallas_call x1, Pallas kernels, run_layer(): pl.pallas_call(functools.partial(layer_kernel, heads, head_size, state_si...  111 us
    ppermute x3, waiting for transfers between devices, body(): arrived.append(lax.ppermute(back[k], 'dp', perm))  22.2 us
    pallas_call x1, Pallas kernels, project(): pl.pallas_call(project_kernel, out_shape=jax.ShapeDtypeStruct((rows, widt...  6.49 us
    ppermute x3, starting transfers between devices, body(): arrived.append(lax.ppermute(back[k], 'dp', perm))  5.76 us
    concatenate x1, local copies, waits for them, and re-layouts, body(): jnp.concatenate([bc_weight[:, :state_size], dt_weight, pad_b, bc_weight[:...  4.14 us
    reshape x1, local copies, waits for them, and re-layouts, body(): outbound = outbound.reshape(shard_count, capacity, inner, state_size)  4.02 us
  transfers between devices with their start and end apart: 7, of which 3 were waited for; matrix products, arithmetic and copies ran while one was open for 17% of the time, Pallas kernels for 57%

profile of v2, /device:TPU:11, one launch (start us, length us, event | category | flops | bytes accessed | tf_op | source)
XLA Modules:
  0.0 196.7 jit_solution(15521869701161418249)
XLA Ops:
  7.2 0.7 collective-permute-start
  8.0 1.0 constant_dynamic-slice_fusion
  8.9 0.3 collective-permute-start.1
  9.3 0.8 select_reduce_fusion
  10.1 0.2 convert_reduce_fusion
  10.4 0.7 and_select_fusion.4
  11.1 0.2 convert_reduce_fusion.1
  11.3 0.7 gather_fusion.1
  12.0 1.3 gather_fusion
  13.3 1.3 copy.21.bias_ref
  14.6 1.3 copy.22.rate_ref
  15.9 1.8 copy.20
  17.7 2.4 %fusion.23 = (bf16[2048,64]{1,0:T(8,128)(2,1)}, bf16[2048,64]{1,0:T(8,128)(2,1)}) fusion(bf16[2048,128]{1,0:T(8,128)(2,1)} %param.15), kind=kLoop, calls=%fused_computation.58 | loop fusion | bytes 1048576 | tf_op jit(solution)/shard_map/slice | solution.py:438
  20.1 1.5 convolution_convert_fusion.2
  21.6 4.0 %reshape.144.outbound_ref = bf16[4,4,512,64]{3,2,1,0:T(8,128)(2,1)} reshape(bf16[16,32768]{1,0:T(8,128)(2,1)} %convolution_convert_fusion.2) | data formatting | bytes 2097152 | tf_op jit(solution)/shard_map/reshape | solution.py:432
  25.6 0.9 broadcast_in_dim.11
  26.5 0.9 broadcast_in_dim.10
  27.4 4.1 %concatenate.10.bd_ref = bf16[2048,256]{1,0:T(8,128)(2,1)} concatenate(bf16[2048,64]{1,0:T(8,128)(2,1)} %get-tuple-element.13, bf16[2048,8]{1,0:T(8,128)(2,1)} %copy.20, bf16[2048,56]{1,0:T(8,128)(2,1)} %broadcast_in_dim.10, bf16[2048,64]{1,0:T(8,128)(2,1)} %get-tuple-element.12, bf16[2048,64]{1,0:T(8,128)(2,1)} %broadcast_in_dim.11), dimensions={1} | concatenate | bytes 2097152 | tf_op jit(solution)/shard_map/concatenate | solution.py:437
  31.5 0.7 pad_add_fusion.scalars
  32.2 111.3 %layer.1 = (bf16[512,2048]{1,0:T(8,128)(2,1)}, bf16[16,512,64]{2,1,0:T(8,128)(2,1)}) custom-call(s32[32]{0:T(128)} %pad_add_fusion.scalars, bf16[4,4,128,512]{3,2,1,0:T(8,128)(2,1)} %bitcast.10, bf16[4,4,512,64]{3,2,1,0:T(8,128)(2,1)} %reshape.144.outbound_ref, bf16[2048,512]{1,0:T(8,128)(2,1)} %x_ref.1, bf16[2048,512]{1,0:T(8,128)(2,1)} %z_ref.1, ...), custom_call_target="tpu_custom_call" | custom-call | flops 42949672960 | bytes 67108864 | tf_op jit(solution)/shard_map/layer/pallas_call | solution.py:306
  143.6 3.7 %reshape.145 = bf16[16,32768]{1,0:T(8,128)(2,1)} reshape(bf16[16,512,64]{2,1,0:T(8,128)(2,1)} %get-tuple-element.5) | data formatting | bytes 2097152 | tf_op jit(solution)/shard_map/reshape | solution.py:465
  147.2 2.7 %convolution_convert_fusion.1 = bf16[16,32768]{1,0:T(8,128)(2,1)} fusion(bf16[16,32768]{1,0:T(8,128)(2,1)} %reshape.145, s32[16]{0:T(128)S(1)} %gather_fusion.1), kind=kOutput, calls=%fused_computation.3 | convolution fusion | flops 17301760 | bytes 2097216 | tf_op jit(solution)/shard_map/dot_general | solution.py:467
  150.0 2.1 %fusion.22 = (bf16[4,32768]{1,0:T(4,128)(2,1)S(1)}, bf16[4,32768]{1,0:T(4,128)(2,1)S(1)}, bf16[4,32768]{1,0:T(4,128)(2,1)S(1)}, bf16[4,32768]{1,0:T(4,128)(2,1)S(1)}) fusion(bf16[16,32768]{1,0:T(8,128)(2,1)} %convolution_convert_fusion.1), kind=kLoop, calls=%fused_computation.57 | loop fusion | bytes 2097152 | tf_op jit(solution)/shard_map/slice | solution.py:468
  152.1 0.1 collective-permute-start.5
  152.1 4.3 %collective-permute-start.4 = (bf16[4,32768]{1,0:T(4,128)(2,1)S(1)}, bf16[4,32768]{1,0:T(4,128)(2,1)S(1)}, u32[]{:S(2)}, u32[]{:S(2)}) collective-permute-start(bf16[4,32768]{1,0:T(4,128)(2,1)S(1)} %get-tuple-element.10), channel_id=1, source_target_pairs={{0,8},{4,12},{8,0},{12,4},{1,9},{5,13},{9,1},{13,5},{2,10},{6,14},... | collective-permute-start | bytes 786440 | tf_op jit(solution)/shard_map/ppermute | solution.py:472
  156.5 1.4 collective-permute-start.3
  157.8 1.6 collective-permute-done.5
  159.5 15.0 %collective-permute-done.4 = bf16[4,32768]{1,0:T(4,128)(2,1)S(1)} collective-permute-done((bf16[4,32768]{1,0:T(4,128)(2,1)S(1)}, bf16[4,32768]{1,0:T(4,128)(2,1)S(1)}, u32[]{:S(2)}, u32[]{:S(2)}) %collective-permute-start.4) | collective-permute-done | bytes 262176 | tf_op jit(solution)/shard_map/ppermute | solution.py:472
  174.5 5.6 %collective-permute-done.3 = bf16[4,32768]{1,0:T(4,128)(2,1)S(1)} collective-permute-done((bf16[4,32768]{1,0:T(4,128)(2,1)S(1)}, bf16[4,32768]{1,0:T(4,128)(2,1)S(1)}, u32[]{:S(2)}, u32[]{:S(2)}) %collective-permute-start.3) | collective-permute-done | bytes 262176 | tf_op jit(solution)/shard_map/ppermute | solution.py:472
  180.0 1.7 convolution_convert_fusion
  181.8 1.6 copy-done.3
  183.4 6.5 %project.1 = bf16[512,2048]{1,0:T(8,128)(2,1)} custom-call(bf16[512,2048]{1,0:T(8,128)(2,1)S(1)} %copy-done.3, bf16[512,2048]{1,0:T(8,128)(2,1)S(1)} %copy-done.1, bf16[512,2048]{1,0:T(8,128)(2,1)S(1)} %collective-permute-done.w1_ref, bf16[512,2048]{1,0:T(8,128)(2,1)S(1)} %copy-done.2, bf16[512,2048]{1,0:T(8,128)(2,1)S(1)} %collective-permute-done.2.w3_ref), custom_call_target="tpu_custom_call" | custom-call | flops 4294967296 | bytes 12582912 | tf_op jit(solution)/shard_map/project/pallas_call | solution.py:363
  (21 shorter events, 0.2 us)
Async XLA Ops:
  7.2 12.9 %copy-start = (bf16[16,32768]{1,0:T(8,128)(2,1)S(1)}, bf16[16,32768]{1,0:T(8,128)(2,1)}, u32[]{:S(2)}) copy-start(bf16[16,32768]{1,0:T(8,128)(2,1)} %param.21) | copy-start | bytes 3145732
  7.2 142.8 %all-gather.2.cloned.1.call-start = ((), (), s32[]{:S(2)}) async-start(), calls=%async_computation | async-start | bytes 2359296 | tf_op jit(solution)/shard_map/all_gather | solution.py:447
  7.2 174.6 %collective-permute-start = (bf16[512,2048]{1,0:T(8,128)(2,1)}, bf16[512,2048]{1,0:T(8,128)(2,1)S(1)}, u32[]{:S(2)}, u32[]{:S(2)}) collective-permute-start(bf16[512,2048]{1,0:T(8,128)(2,1)} %w0_ref.1), channel_id=1, source_target_pairs={{0,1},{1,0},{2,3},{3,2},{4,5},{5,4},{6,7},{7,6},{8,9},{9,8},{10,11... | collective-permute-start | bytes 6291464 | tf_op jit(solution)/shard_map/ppermute | solution.py:411
  8.9 23.3 %collective-permute-start.1 = (bf16[64,2048]{1,0:T(8,128)(2,1)S(1)}, bf16[64,2048]{1,0:T(8,128)(2,1)}, u32[]{:S(2)}, u32[]{:S(2)}) collective-permute-start(bf16[64,2048]{1,0:T(8,128)(2,1)S(1)} %constant_dynamic-slice_fusion), channel_id=1, source_target_pairs={{0,2},{1,3},{2,0},{3,1},{4,6},{5,7},{6,4},{7,5},{8,10},{9,11},{10,... | collective-permute-start | bytes 786440 | tf_op jit(solution)/shard_map/ppermute | solution.py:411
  150.0 31.8 %collective-permute-start.2 = (bf16[512,2048]{1,0:T(8,128)(2,1)}, bf16[512,2048]{1,0:T(8,128)(2,1)S(1)}, u32[]{:S(2)}, u32[]{:S(2)}) collective-permute-start(bf16[512,2048]{1,0:T(8,128)(2,1)} %all-gather.2.cloned.1.call-done.w2_ref), channel_id=1, source_target_pairs={{0,1},{1,0},{2,3},{3,2},{4,5},{5,4},{6,7},{7,6},{8,9},{9,8},{10,11... | collective-permute-start | bytes 6291464 | tf_op jit(solution)/shard_map/ppermute | solution.py:411
  150.0 31.8 %copy-start.2 = (bf16[512,2048]{1,0:T(8,128)(2,1)S(1)}, bf16[512,2048]{1,0:T(8,128)(2,1)}, u32[]{:S(2)}) copy-start(bf16[512,2048]{1,0:T(8,128)(2,1)} %all-gather.2.cloned.1.call-done.w2_ref) | copy-start | bytes 6291460
  152.1 29.7 %copy-start.1 = (bf16[512,2048]{1,0:T(8,128)(2,1)S(1)}, bf16[512,2048]{1,0:T(8,128)(2,1)}, u32[]{:S(2)}) copy-start(bf16[512,2048]{1,0:T(8,128)(2,1)} %w0_ref.1) | copy-start | bytes 6291460
  152.1 7.4 %collective-permute-start.5 = (bf16[4,32768]{1,0:T(4,128)(2,1)S(1)}, bf16[4,32768]{1,0:T(4,128)(2,1)S(1)}, u32[]{:S(2)}, u32[]{:S(2)}) collective-permute-start(bf16[4,32768]{1,0:T(4,128)(2,1)S(1)} %get-tuple-element.9), channel_id=1, source_target_pairs={{0,4},{4,8},{8,12},{12,0},{1,5},{5,9},{9,13},{13,1},{2,6},{6,10},{... | collective-permute-start | bytes 786440 | tf_op jit(solution)/shard_map/ppermute | solution.py:472
  152.1 22.3 %collective-permute-start.4 = (bf16[4,32768]{1,0:T(4,128)(2,1)S(1)}, bf16[4,32768]{1,0:T(4,128)(2,1)S(1)}, u32[]{:S(2)}, u32[]{:S(2)}) collective-permute-start(bf16[4,32768]{1,0:T(4,128)(2,1)S(1)} %get-tuple-element.10), channel_id=1, source_target_pairs={{0,8},{4,12},{8,0},{12,4},{1,9},{5,13},{9,1},{13,5},{2,10},{6,14},... | collective-permute-start | bytes 786440 | tf_op jit(solution)/shard_map/ppermute | solution.py:472
  156.5 23.6 %collective-permute-start.3 = (bf16[4,32768]{1,0:T(4,128)(2,1)S(1)}, bf16[4,32768]{1,0:T(4,128)(2,1)S(1)}, u32[]{:S(2)}, u32[]{:S(2)}) collective-permute-start(bf16[4,32768]{1,0:T(4,128)(2,1)S(1)} %get-tuple-element.11), channel_id=1, source_target_pairs={{0,12},{4,0},{8,4},{12,8},{1,13},{5,1},{9,5},{13,9},{2,14},{6,2},{... | collective-permute-start | bytes 786440 | tf_op jit(solution)/shard_map/ppermute | solution.py:472
  181.8 1.6 copy-start.3
Sparse Core Ops, SparseCore 0:
  32.3 77.8 all-gather.1

commit v3 on v2

v3 whole, which is shorter than its diff:
```python
import functools

import jax
import jax.numpy as jnp
from jax import lax
from jax.experimental import pallas as pl
from jax.experimental.pallas import tpu as pltpu
from jax.sharding import PartitionSpec as P

F32 = jnp.float32
BF16 = jnp.bfloat16


def rank_within(keys, order):
    earlier = (keys[None, :] == keys[:, None]) & (order[None, :] < order[:, None])
    return jnp.sum(earlier.astype(jnp.int32), axis=1)


def xor_place(me, mask):
    return lax.rem(lax.rem(me, 2) + mask % 2, 2) + 2 * lax.rem(me // 2 + mask // 2, 2)


def layer_kernel(
    heads,
    head_size,
    state_size,
    chunks,
    parts,
    shards,
    scalars,
    tokens_ref,
    store_ref,
    x_ref,
    z_ref,
    bc_ref,
    dtw_ref,
    bias_ref,
    rate_ref,
    gain_ref,
    outw_ref,
    out_ref,
    new_store_ref,
    own,
    sib,
    far,
    diag,
    outbound,
    inbound,
    state_ref,
    outgoing,
    returned,
    acc_ref,
    normed_ref,
    own_sum,
    far_part,
    pair_out,
    pair_in,
    far_out,
    far_in,
    own_sem,
    sib_send,
    sib_recv,
    far_send,
    far_recv,
    diag_send,
    diag_recv,
    store_send,
    store_recv,
    back_send,
    back_recv,
    pair_send,
    pair_recv,
    sum_send,
    sum_recv,
):
    slots = tokens_ref.shape[2]
    depth = tokens_ref.shape[3]
    inner = heads * head_size
    sessions = chunks * parts
    capacity = outbound.shape[1]
    me = lax.axis_index("mp")
    dp = lax.axis_index("dp")
    MESH = pl.DeviceIdType.MESH

    barrier = pltpu.get_barrier_semaphore()
    for mask in range(1, parts):
        pl.semaphore_signal(
            barrier, inc=1, device_id={"mp": xor_place(me, mask)}, device_id_type=MESH
        )
    for k in range(1, shards):
        pl.semaphore_signal(
            barrier, inc=1, device_id={"dp": lax.rem(dp + k, shards)}, device_id_type=MESH
        )
    pl.semaphore_wait(barrier, parts - 1 + shards - 1)

    def remote(src, dst, send, recv, device):
        return pltpu.make_async_remote_copy(
            src_ref=src,
            dst_ref=dst,
            send_sem=send,
            recv_sem=recv,
            device_id=device,
            device_id_type=MESH,
        )

    def far_copy(j):
        return remote(
            tokens_ref.at[:, j], far.at[j], far_send.at[j], far_recv.at[j], {"mp": xor_place(me, 2)}
        )

    def sib_copy(j):
        return remote(
            tokens_ref.at[:, j], sib.at[j], sib_send.at[j], sib_recv.at[j], {"mp": xor_place(me, 1)}
        )

    def diag_copy(j):
        return remote(
            far.at[j], diag.at[j], diag_send.at[j], diag_recv.at[j], {"mp": xor_place(me, 1)}
        )

    def own_copy(j):
        return pltpu.make_async_copy(tokens_ref.at[:, j], own.at[j], own_sem.at[j])

    def store_copy(k):
        return remote(
            outbound.at[k],
            inbound.at[k],
            store_send.at[k],
            store_recv.at[k],
            {"dp": lax.rem(dp + k, shards)},
        )

    def back_copy(k):
        return remote(
            outgoing.at[k],
            returned.at[k],
            back_send.at[k],
            back_recv.at[k],
            {"dp": lax.rem(dp + shards - k, shards)},
        )

    def pair_copy(j):
        return remote(
            pair_out.at[j], pair_in.at[j], pair_send.at[j], pair_recv.at[j], {"mp": xor_place(me, 1)}
        )

    def sum_copy(j):
        return remote(
            far_out.at[j], far_in.at[j], sum_send.at[j], sum_recv.at[j], {"mp": xor_place(me, 2)}
        )

    ahead = min(2, chunks)
    for j in range(ahead):
        far_copy(j).start()
    for j in range(chunks):
        own_copy(j).start()
        sib_copy(j).start()

    def fill_outbound(k):
        for c in range(capacity):
            outbound[k, c] = store_ref[scalars[2 * sessions + k * capacity + c]]

    for k in range(1, shards):
        fill_outbound(k)
        store_copy(k).start()
    for c in range(capacity):
        inbound[0, c] = store_ref[scalars[2 * sessions + c]]

    eye = lax.broadcasted_iota(jnp.int32, (heads, heads), 0) == lax.broadcasted_iota(
        jnp.int32, (heads, heads), 1
    )
    rate_col = jnp.sum(jnp.where(eye, rate_ref[...], 0.0), axis=1, keepdims=True)
    bias_col = jnp.sum(jnp.where(eye, bias_ref[...], 0.0), axis=1, keepdims=True)
    lane = lax.broadcasted_iota(jnp.int32, (slots, slots), 1)
    row = lax.broadcasted_iota(jnp.int32, (slots, slots), 0)
    causal = row >= lane
    low = lane < head_size
    lane8 = lax.broadcasted_iota(jnp.int32, (heads, slots), 1)
    pair = 2 * head_size
    tile = min(512, out_ref.shape[1])
    spread = (row == 2 * (lane % head_size) + lane // head_size).astype(BF16)

    def session(j, step):
        place = lax.rem(lax.rem(me, 2) + lax.rem(step, 2), 2) + 2 * lax.rem(me // 2 + step // 2, 2)
        here = pl.ds(pl.multiple_of(place * slots, slots), slots)
        index = place * chunks + j
        count = scalars[index]
        spot = scalars[sessions + index]
        spot_k = spot // capacity
        spot_c = spot - spot_k * capacity
        bc = acc_ref[here, 2 * inner : 2 * inner + 2 * state_size]
        b_bf = bc[:, :state_size].astype(BF16)
        b_f32 = b_bf.astype(F32)
        c_bf = bc[:, state_size:].astype(BF16)
        slab = acc_ref[here, 2 * inner + 2 * state_size : 2 * inner + 2 * state_size + 128]
        raw = slab.T[:heads, :] + bias_col
        dt_t = jnp.maximum(raw, 0.0) + jnp.log1p(jnp.exp(-jnp.abs(raw)))
        dt_t = jnp.where(lane8 < count, dt_t, 0.0)
        cum_t = dt_t * rate_col
        shift = 1
        while shift < slots:
            moved = pltpu.roll(cum_t, shift, axis=1)
            cum_t = cum_t + jnp.where(lane8 >= shift, moved, 0.0)
            shift *= 2
        last = cum_t[:, slots - 1 : slots]
        weigh_t = jnp.exp(cum_t - last) * dt_t
        fade_t = jnp.exp(-cum_t)
        stacked = jnp.concatenate(
            [cum_t, weigh_t, fade_t, jnp.zeros((slots - 3 * heads, slots), F32)], axis=0
        ).T
        scores = lax.dot_general(
            c_bf, b_bf, (((1,), (1,)), ((), ())), preferred_element_type=F32
        )
        gated_parts = []
        squares = None
        for g in range(heads // 2):
            cols = slice(g * pair, (g + 1) * pair)
            xs = acc_ref[here, cols].astype(BF16)
            zs = acc_ref[here, inner + g * pair : inner + (g + 1) * pair].astype(BF16).astype(F32)
            split = jnp.concatenate(
                [jnp.where(low, xs, jnp.zeros((), BF16)), jnp.where(low, jnp.zeros((), BF16), xs)],
                axis=0,
            )
            mixes = []
            weighed = []
            for h in (2 * g, 2 * g + 1):
                gaps = jnp.where(causal, cum_t[h : h + 1, :] - stacked[:, h : h + 1], -1e30)
                mixes.append((jnp.exp(gaps) * dt_t[h : h + 1, :] * scores).astype(BF16))
                weighed.append((b_f32 * stacked[:, heads + h : heads + h + 1]).astype(BF16))
            y = jnp.dot(jnp.concatenate(mixes, axis=1), split, preferred_element_type=F32)
            rows = slice(g * head_size, (g + 1) * head_size)
            kept = inbound[spot_k, spot_c, rows, :]
            halves = jnp.concatenate([kept[:, :state_size], kept[:, state_size:]], axis=0)
            start = jnp.dot(spread, halves, preferred_element_type=F32).astype(BF16)
            carried = lax.dot_general(
                c_bf, start, (((1,), (1,)), ((), ())), preferred_element_type=F32
            )
            fade0 = stacked[:, 2 * heads + 2 * g : 2 * heads + 2 * g + 1]
            fade1 = stacked[:, 2 * heads + 2 * g + 1 : 2 * heads + 2 * g + 2]
            y = y + carried * jnp.where(low, fade0, fade1)
            grown = lax.dot_general(
                jnp.dot(split, spread, preferred_element_type=F32).astype(BF16),
                jnp.concatenate(weighed, axis=0),
                (((0,), (0,)), ((), ())),
                preferred_element_type=F32,
            )
            keep = jnp.where(
                row[:head_size] < head_size // 2,
                fade_t[2 * g : 2 * g + 1, slots - 1 : slots],
                fade_t[2 * g + 1 : 2 * g + 2, slots - 1 : slots],
            )
            grown = jnp.concatenate([grown[:head_size], grown[head_size:]], axis=1)
            state_ref[index, rows, :] = (keep * kept.astype(F32) + grown).astype(BF16)
            gated = y * (zs * jax.nn.sigmoid(zs))
            part = jnp.sum(gated * gated, axis=1, keepdims=True)
            squares = part if squares is None else squares + part
            gated_parts.append(gated)
        scale = lax.rsqrt(squares * (1.0 / inner) + 1e-05)
        scale = jnp.where(row[:, :1] < count, scale, 0.0)
        for g in range(heads // 2):
            cols = slice(g * pair, (g + 1) * pair)
            normed_ref[pl.ds(pl.multiple_of(step * slots, slots), slots), cols] = (gated_parts[g] * scale * gain_ref[:, cols]).astype(BF16)

    def compute(j):
        own_copy(j).wait()
        sib_copy(j).wait_recv()
        diag_copy(j).wait_recv()
        pieces = []
        for step, ref in enumerate((own, sib, far, diag)):
            rows = pl.ds(pl.multiple_of(xor_place(me, step) * depth, depth), depth)
            pieces.append((ref[j].reshape(parts * slots, depth), rows))
        base = 0
        for weight in (x_ref, z_ref, bc_ref, dtw_ref):
            width = weight.shape[1]
            total = None
            for values, rows in pieces:
                piece = jnp.dot(values, weight[rows, :], preferred_element_type=F32)
                total = piece if total is None else total + piece
            if width < 128:
                total = jnp.concatenate(
                    [total, jnp.zeros((total.shape[0], 128 - width), F32)], axis=1
                )
                width = 128
            acc_ref[:, base : base + width] = total
            base += width

        @pl.when(j > 0)
        def _():
            combine(j - 1)

        def run_session(step, carry):
            session(j, step)
            return carry

        lax.fori_loop(0, parts, run_session, 0)

        @pl.loop(0, out_ref.shape[1] // tile)
        def _(t):
            cols = pl.ds(pl.multiple_of(t * tile, tile), tile)
            part = jnp.dot(normed_ref[...], outw_ref[:, cols], preferred_element_type=F32)
            own_sum[j, :, cols] = part[:slots]
            pair_out[j, 0, :, cols] = part[slots : 2 * slots].astype(BF16)
            far_part[:, cols] = part[2 * slots : 3 * slots]
            pair_out[j, 1, :, cols] = part[3 * slots :].astype(BF16)

        pair_copy(j).start()

    def combine(j):
        pair_copy(j).wait_recv()
        far_out[j] = (far_part[...] + pair_in[j, 1].astype(F32)).astype(BF16)
        sum_copy(j).start()

    def round_trip(j, carry):
        @pl.when(j < chunks)
        def _():
            far_copy(j).wait_recv()
            diag_copy(j).start()

        @pl.when(j + ahead < chunks)
        def _():
            far_copy(j + ahead).start()

        @pl.when(j == 1)
        def _():
            for k in range(1, shards):
                store_copy(k).wait_recv()

        @pl.when(j > 0)
        def _():
            compute(j - 1)

        return carry

    lax.fori_loop(0, chunks + 1, round_trip, 0)

    for k in range(1, shards):
        for c in range(capacity):
            outgoing[k, c] = state_ref[scalars[2 * sessions + shards * capacity + k * capacity + c]]
        back_copy(k).start()
    for c in range(capacity):
        returned[0, c] = state_ref[scalars[2 * sessions + shards * capacity + c]]
    combine(chunks - 1)

    for j in range(chunks):
        sum_copy(j).wait_recv()
        rows = slice(j * slots, (j + 1) * slots)
        out_ref[rows, :] = (
            own_sum[j] + pair_in[j, 0].astype(F32) + far_in[j].astype(F32)
        ).astype(BF16)

    for k in range(1, shards):
        back_copy(k).wait_recv()
    for r in range(sessions):
        spot = scalars[2 * sessions + 2 * shards * capacity + r]
        spot_k = spot // capacity
        new_store_ref[r] = returned[spot_k, spot - spot_k * capacity]

    for j in range(chunks):
        far_copy(j).wait_send()
        sib_copy(j).wait_send()
        diag_copy(j).wait_send()
        pair_copy(j).wait_send()
        sum_copy(j).wait_send()
    for k in range(1, shards):
        store_copy(k).wait_send()
        back_copy(k).wait_send()


def run_layer(scalars, tokens4, store, weights, params, out_weight, sizes, shards, capacity):
    heads, head_size, state_size = sizes
    parts, chunks, slots, depth = tokens4.shape
    inner = heads * head_size
    width = 2 * inner + 2 * state_size + 128
    rows = parts * slots
    model = out_weight.shape[1]
    packed = store.shape[1:]
    vmem = pl.BlockSpec(memory_space=pltpu.VMEM)
    hbm = pl.BlockSpec(memory_space=pl.ANY)
    dma = pltpu.SemaphoreType.DMA
    block = pltpu.VMEM((chunks, parts, slots, depth), BF16)
    exchange = pltpu.VMEM((shards, capacity) + packed, BF16)
    return pl.pallas_call(
        functools.partial(layer_kernel, heads, head_size, state_size, chunks, parts, shards),
        out_shape=(
            jax.ShapeDtypeStruct((chunks * slots, model), BF16),
            jax.ShapeDtypeStruct(store.shape, BF16),
        ),
        in_specs=[pl.BlockSpec(memory_space=pltpu.SMEM), hbm] + [vmem] * 9,
        out_specs=(vmem, vmem),
        scratch_shapes=[
            block,
            block,
            block,
            block,
            exchange,
            exchange,
            pltpu.VMEM((chunks * parts,) + packed, BF16),
            exchange,
            exchange,
            pltpu.VMEM((rows, width), F32),
            pltpu.VMEM((rows, inner), BF16),
            pltpu.VMEM((chunks, slots, model), F32),
            pltpu.VMEM((slots, model), F32),
            pltpu.VMEM((chunks, 2, slots, model), BF16),
            pltpu.VMEM((chunks, 2, slots, model), BF16),
            pltpu.VMEM((chunks, slots, model), BF16),
            pltpu.VMEM((chunks, slots, model), BF16),
        ]
        + [dma((chunks,))] * 7
        + [dma((shards,))] * 4
        + [dma((chunks,))] * 4,
        compiler_params=pltpu.CompilerParams(
            vmem_limit_bytes=62 * 1024 * 1024, collective_id=0, has_side_effects=True
        ),
        cost_estimate=pl.CostEstimate(
            flops=2 * chunks * rows * 4 * depth * width * 4,
            bytes_accessed=64 * 1024 * 1024,
            transcendentals=chunks * rows * heads * slots,
        ),
        name="layer",
    )(scalars, tokens4, store, *weights, *params, out_weight)


def body(
    tokens,
    x_weight,
    z_weight,
    bc_weight,
    dt_weight,
    dt_bias,
    decay_rate,
    norm_gain,
    out_weight,
    store_states,
    home_rows,
    event_counts,
):
    shard_count = lax.axis_size("dp")
    parts = lax.axis_size("mp")
    me = lax.axis_index("dp")
    sessions = store_states.shape[0]
    state_width = store_states.shape[1]
    capacity = max(2, (sessions + shard_count - 1) // shard_count)
    slot_count = shard_count * capacity
    heads = dt_bias.shape[0]
    inner = x_weight.shape[1]
    head_size = inner // heads
    state_size = bc_weight.shape[1] // 2
    depth = tokens.shape[1]
    slots = tokens.shape[0] // sessions
    chunks = sessions // parts

    tokens4 = tokens.reshape(parts, chunks, slots, depth)

    positions = jnp.arange(sessions, dtype=jnp.int32)
    store_rows = me * sessions + positions
    everyone = jnp.arange(home_rows.shape[0], dtype=jnp.int32)
    owner = jnp.sum(
        (home_rows[None, :] == store_rows[:, None]).astype(jnp.int32) * everyone[None, :], axis=1
    )
    server = owner // sessions
    to_server = (server - me + shard_count) % shard_count
    row_slot = to_server * capacity + rank_within(server, positions)
    wanted = lax.dynamic_slice_in_dim(home_rows, me * sessions, sessions)
    home_shard = wanted // sessions
    from_home = (me - home_shard + shard_count) % shard_count
    session_slot = from_home * capacity + rank_within(home_shard, wanted % sessions)

    all_slots = jnp.arange(slot_count, dtype=jnp.int32)

    def holder(slot_of):
        chosen = slot_of[None, :] == all_slots[:, None]
        return jnp.sum(chosen.astype(jnp.int32) * positions[None, :], axis=1)

    scalars = jnp.concatenate(
        [event_counts, session_slot, holder(row_slot), holder(session_slot), row_slot]
    )
    out_sum, new_store = run_layer(
        scalars,
        tokens4,
        store_states.reshape(sessions, state_width // (2 * state_size), 2 * state_size),
        (x_weight, z_weight, bc_weight, dt_weight),
        (dt_bias[None, :], decay_rate[None, :], norm_gain[None, :]),
        out_weight,
        (heads, head_size, state_size),
        shard_count,
        capacity,
    )
    new_store = new_store.reshape(sessions, state_width)
    return (out_sum, new_store)


def solution(mesh):
    return jax.shard_map(
        body,
        mesh=mesh,
        in_specs=(
            P(("groups", "dp"), "mp"),
            P(None, "mp"),
            P(None, "mp"),
            P(None, "mp"),
            P(None, "mp"),
            P("mp"),
            P("mp"),
            P("mp"),
            P("mp", None),
            P(("groups", "dp"), "mp"),
            P("groups"),
            P(("groups", "dp")),
        ),
        out_specs=(P(("groups", "dp", "mp"), None), P(("groups", "dp"), "mp")),
        check_vma=False,
    )
```

time: 197 us -> 125 us (0.63)
  the two profiles are of different devices: /device:TPU:11 before, /device:TPU:0 now
where the time goes in v3:
time: 125 us
  Pallas kernels  112 us (90%)
  local copies, waits for them, and re-layouts  9.71 us (8%)
  other arithmetic  2.22 us (2%)
    pallas_call x1, Pallas kernels, run_layer(): pl.pallas_call(functools.partial(layer_kernel, heads, head_size, state_si...  112 us
    unnamed x6, local copies, waits for them, and re-layouts  8.49 us

profile of v3, /device:TPU:0, one launch (start us, length us, event | category | flops | bytes accessed | tf_op | source)
XLA Modules:
  0.0 124.5 jit_solution(7726367694302975359)
XLA Ops:
  0.6 0.8 select_reduce_fusion.2
  1.5 0.2 convert_reduce_fusion
  1.7 0.7 and_select_fusion.4
  2.4 0.2 convert_reduce_fusion.1
  2.6 0.1 select_reduce_fusion
  2.8 0.1 select_reduce_fusion.1
  2.9 1.2 concatenate.3.scalars
  4.1 1.8 %copy.15.dtw_ref = bf16[2048,8]{1,0:T(8,128)(2,1)} copy(bf16[2048,8]{0,1:T(8,128)(2,1)} %param.16) | data formatting | bytes 65536 | tf_op args[4]
  5.8 2.4 %copy.16 = bf16[2,8,256,128]{3,2,1,0:T(8,128)(2,1)} copy(bf16[2,8,256,128]{3,1,2,0:T(8,128)(2,1)} %bitcast.10) | data formatting | bytes 2097152
  8.2 111.9 %layer.1 = (bf16[512,2048]{1,0:T(8,128)(2,1)}, bf16[16,256,128]{2,1,0:T(8,128)(2,1)}) custom-call(s32[80]{0:T(128)} %concatenate.3.scalars, bf16[4,4,128,512]{3,2,1,0:T(8,128)(2,1)} %bitcast.14, bf16[16,256,128]{2,1,0:T(8,128)(2,1)} %bitcast.13, bf16[2048,512]{1,0:T(8,128)(2,1)} %x_ref.1, bf16[2048,512]{1,0:T(8,128)(2,1)} %z_ref.1, ...), custom_call_target="tpu_custom_call" | custom-call | flops 42949672960 | bytes 67108864 | tf_op jit(solution)/shard_map/layer/pallas_call | solution.py:382
  120.2 0.0 copy-start
  120.2 3.0 %copy.19 = bf16[2,8,256,128]{3,1,2,0:T(8,128)(2,1)} copy(bf16[2,8,256,128]{3,2,1,0:T(8,128)(2,1)} %bitcast.12) | data formatting | bytes 2097152
  123.2 0.0 copy-done
  123.2 1.3 %copy.21 = bf16[512,2048]{1,0:T(8,128)(2,1)} copy(bf16[512,2048]{1,0:T(8,128)(2,1)S(1)} %copy-done) | data formatting | bytes 4194304
  (4 shorter events, 0.0 us)
Async XLA Ops:
  120.2 3.0 %copy-start = (bf16[512,2048]{1,0:T(8,128)(2,1)S(1)}, bf16[512,2048]{1,0:T(8,128)(2,1)}, u32[]{:S(2)}) copy-start(bf16[512,2048]{1,0:T(8,128)(2,1)} %get-tuple-element.12) | copy-start | bytes 6291460

commit v4 on v3

--- a/solution.py
+++ b/solution.py
@@ -177,6 +177,7 @@
     low = lane < head_size
     lane8 = lax.broadcasted_iota(jnp.int32, (heads, slots), 1)
     pair = 2 * head_size
+    kept_at = 2 * sessions + shards * capacity
     tile = min(512, out_ref.shape[1])
     spread = (row == 2 * (lane % head_size) + lane // head_size).astype(BF16)
 
@@ -261,7 +262,7 @@
             cols = slice(g * pair, (g + 1) * pair)
             normed_ref[pl.ds(pl.multiple_of(step * slots, slots), slots), cols] = (gated_parts[g] * scale * gain_ref[:, cols]).astype(BF16)
 
-    def compute(j):
+    def project(j):
         own_copy(j).wait()
         sib_copy(j).wait_recv()
         diag_copy(j).wait_recv()
@@ -284,15 +285,24 @@
             acc_ref[:, base : base + width] = total
             base += width
 
+    def run_sessions(j):
         @pl.when(j > 0)
         def _():
             combine(j - 1)
 
-        def run_session(step, carry):
-            session(j, step)
+        def two_sessions(step, carry):
+            session(j, 2 * step)
+            session(j, 2 * step + 1)
             return carry
 
-        lax.fori_loop(0, parts, run_session, 0)
+        lax.fori_loop(0, parts // 2, two_sessions, 0)
+
+        @pl.when(j == chunks - 1)
+        def _():
+            for k in range(1, shards):
+                for c in range(capacity):
+                    outgoing[k, c] = state_ref[scalars[kept_at + k * capacity + c]]
+                back_copy(k).start()
 
         @pl.loop(0, out_ref.shape[1] // tile)
         def _(t):
@@ -327,18 +337,18 @@
 
         @pl.when(j > 0)
         def _():
-            compute(j - 1)
+            run_sessions(j - 1)
+
+        @pl.when(j < chunks)
+        def _():
+            project(j)
 
         return carry
 
     lax.fori_loop(0, chunks + 1, round_trip, 0)
 
-    for k in range(1, shards):
-        for c in range(capacity):
-            outgoing[k, c] = state_ref[scalars[2 * sessions + shards * capacity + k * capacity + c]]
-        back_copy(k).start()
     for c in range(capacity):
-        returned[0, c] = state_ref[scalars[2 * sessions + shards * capacity + c]]
+        returned[0, c] = state_ref[scalars[kept_at + c]]
     combine(chunks - 1)
 
     for j in range(chunks):

time: 125 us -> 120 us (0.960)
  Pallas kernels: 112 us -> 107 us
    pallas_call x1, Pallas kernels: 112 us -> 107 us  [run_layer(): pl.pallas_call(functools.partial(layer_kernel, heads, head_size, state_si...]
where the time goes in v4:
time: 120 us; the launch traced here: 119 us
  Pallas kernels  107 us (89%)
  local copies, waits for them, and re-layouts  9.71 us (8%)
  other arithmetic  2.22 us (2%)
    pallas_call x1, Pallas kernels, run_layer(): pl.pallas_call(functools.partial(layer_kernel, heads, head_size, state_si...  107 us
    unnamed x6, local copies, waits for them, and re-layouts  8.49 us

profile of v4, /device:TPU:0, one launch (start us, length us, event | category | flops | bytes accessed | tf_op | source)
XLA Modules:
  0.0 119.5 jit_solution(1384459084405655463)
XLA Ops:
  0.6 0.8 select_reduce_fusion.2
  1.5 0.2 convert_reduce_fusion
  1.7 0.7 and_select_fusion.4
  2.4 0.2 convert_reduce_fusion.1
  2.6 0.1 select_reduce_fusion
  2.8 0.1 select_reduce_fusion.1
  2.9 1.2 %concatenate.3.scalars = s32[80]{0:T(128)} concatenate(s32[16]{0:T(128)} %param.23, s32[16]{0:T(128)S(1)} %get-tuple-element.8, s32[16]{0:T(128)S(1)} %select_reduce_fusion.1, s32[16]{0:T(128)S(1)} %select_reduce_fusion, s32[16]{0:T(128)S(1)} %get-tuple-element.9), dimensions={0} | concatenate | bytes 640 | tf_op jit(solution)/shard_map/concatenate | solution.py:485
  4.1 1.8 %copy.15.dtw_ref = bf16[2048,8]{1,0:T(8,128)(2,1)} copy(bf16[2048,8]{0,1:T(8,128)(2,1)} %param.16) | data formatting | bytes 65536 | tf_op args[4]
  5.8 2.4 %copy.16 = bf16[2,8,256,128]{3,2,1,0:T(8,128)(2,1)} copy(bf16[2,8,256,128]{3,1,2,0:T(8,128)(2,1)} %bitcast.10) | data formatting | bytes 2097152
  8.2 106.9 %layer.1 = (bf16[512,2048]{1,0:T(8,128)(2,1)}, bf16[16,256,128]{2,1,0:T(8,128)(2,1)}) custom-call(s32[80]{0:T(128)} %concatenate.3.scalars, bf16[4,4,128,512]{3,2,1,0:T(8,128)(2,1)} %bitcast.14, bf16[16,256,128]{2,1,0:T(8,128)(2,1)} %bitcast.13, bf16[2048,512]{1,0:T(8,128)(2,1)} %x_ref.1, bf16[2048,512]{1,0:T(8,128)(2,1)} %z_ref.1, ...), custom_call_target="tpu_custom_call" | custom-call | flops 42949672960 | bytes 67108864 | tf_op jit(solution)/shard_map/layer/pallas_call | solution.py:392
  115.1 0.0 copy-start
  115.1 3.0 %copy.19 = bf16[2,8,256,128]{3,1,2,0:T(8,128)(2,1)} copy(bf16[2,8,256,128]{3,2,1,0:T(8,128)(2,1)} %bitcast.12) | data formatting | bytes 2097152
  118.2 0.0 copy-done
  118.2 1.3 %copy.21 = bf16[512,2048]{1,0:T(8,128)(2,1)} copy(bf16[512,2048]{1,0:T(8,128)(2,1)S(1)} %copy-done) | data formatting | bytes 4194304
  (4 shorter events, 0.0 us)
Async XLA Ops:
  115.1 3.0 %copy-start = (bf16[512,2048]{1,0:T(8,128)(2,1)S(1)}, bf16[512,2048]{1,0:T(8,128)(2,1)}, u32[]{:S(2)}) copy-start(bf16[512,2048]{1,0:T(8,128)(2,1)} %get-tuple-element.12) | copy-start | bytes 6291460
